TPU v7x, 256 devices: a whole 4x4x8 slice. The times are simulated.
256 devices in a mesh: box: 64 (over x, z, core), col: 4 (over y).
Axes of the slice: x: 4, y: 4, z: 8, core: 2. Of those that a mesh axis runs over, the one named last changes fastest.
Arguments:
- child_maps: float32 [64, 1536, 1536], P('box', None, 'col'), may hold values from -13 to 14, as said below
- iface_one: int32 [64, 512], P('box'), may hold values from 0 to 1535, as said below
- iface_two: int32 [32, 512], replicated, may hold values from 0 to 3071, as said below
Outputs:
- parent_two: float32 [64, 6144, 1536], P('box', None, 'col')
Inputs may be any that keep to these rules, and one draw needn't show every extreme that they name: `child_maps`: every child map is symmetric and positive definite. `iface_one`: row c lists 512 distinct points of child c; rows 2k and 2k+1 list the same physical points in the same order. `iface_two`: row p lists 512 distinct points of the first-level parent of children 2p and 2p+1 (points of child 2p+1 counted from 1536), none of them listed in iface_one for those children: first 256 points of child 2p, then 256 of child 2p+1. Rows 2j and 2j+1 list the same physical points in the same order.
All inputs are finite; a program needn't handle non-finite values.
Results may differ from a plain program's by a relative error of at most 0.00005.
Values sent between devices are 32-bit elements; how exact they have to be, the bound alone decides.
No kernel may reach another device: no remote copies, remote signals or barrier semaphores. Data moves between devices by JAX's collectives and lax.ppermute only.
A program may use at most 128 MiB of HBM per device.

v0:
```python
import functools

import jax
import jax.numpy as jnp
from jax import lax
from jax.experimental import pallas as pl
from jax.experimental.pallas import tpu as pltpu
from jax.sharding import PartitionSpec as P

F32 = jnp.float32
BF16 = jnp.bfloat16
HI = lax.Precision.HIGHEST
COLS = 4
IFACE = 512
HALF = 256
EDGE = IFACE + HALF
PARTS = EDGE // HALF


PER = 4

VMEM = pl.BlockSpec(memory_space=pltpu.VMEM)
SMEM = pl.BlockSpec(memory_space=pltpu.SMEM)
ANY = pl.BlockSpec(memory_space=pl.ANY)


def call(body, outs, n_smem, n_in, flops, nbytes, scratch=()):
    return pl.pallas_call(
        body,
        out_shape=outs,
        in_specs=[SMEM] * n_smem + [VMEM] * n_in,
        out_specs=jax.tree.map(lambda _: VMEM, outs),
        scratch_shapes=scratch,
        cost_estimate=pl.CostEstimate(flops=flops, bytes_accessed=nbytes, transcendentals=0),
        compiler_params=pltpu.CompilerParams(vmem_limit_bytes=20 * 2**20),
    )


def shape(*dims):
    return jax.ShapeDtypeStruct(dims, F32)


def lane_of(v, j):
    return jnp.broadcast_to(v[:, j : j + 1], v.shape)


def row_of(v, r):
    return jnp.broadcast_to(v[r : r + 1, :], v.shape)


def eliminate_eight(rows, p, lane, sub):
    off = 8 * p
    full = [row_of(rows[p], k) for k in range(8)]
    e = {(k, j): lane_of(full[k], off + j) for k in range(8) for j in range(k, 8)}
    rest = {i: [lane_of(rows[i], off + j) for j in range(8)] for i in range(16) if i != p}
    inside = (lane >= off) & (lane < off + 8)
    full = [jnp.where(inside, jnp.where(lane == off + k, 1.0, 0.0), full[k]) for k in range(8)]
    low, inv = {}, []
    for k in range(8):
        inv.append(1.0 / e[k, k])
        for r in range(k + 1, 8):
            low[r, k] = e[k, r] * inv[k]
            full[r] = full[r] - low[r, k] * full[k]
        for r in range(k + 1, 8):
            for j in range(r, 8):
                e[r, j] = e[r, j] - low[r, k] * e[k, j]
    full = [full[k] * inv[k] for k in range(8)]
    for k in range(7, 0, -1):
        for r in range(k):
            full[r] = full[r] - low[k, r] * full[k]
    top = full[0]
    for k in range(1, 8):
        top = jnp.where(sub == k, full[k], top)
    out = list(rows)
    out[p] = top
    for i, c in rest.items():
        t = [c[j] * full[j] for j in range(8)]
        s = ((t[0] + t[1]) + (t[2] + t[3])) + ((t[4] + t[5]) + (t[6] + t[7]))
        out[i] = jnp.where(inside, 0.0, rows[i]) - s
    return out


def inverse_128(a):
    lane = lax.broadcasted_iota(jnp.int32, (8, 128), 1)
    sub = lax.broadcasted_iota(jnp.int32, (8, 128), 0)

    def some(_, rows):
        for p in range(PER):
            rows = eliminate_eight(rows, p, lane, sub)
        rows = [pltpu.roll(v, 128 - 8 * PER, 1) for v in rows]
        return tuple(rows[PER:] + rows[:PER])

    rows = lax.fori_loop(0, 16 // PER, some, tuple(a[8 * i : 8 * i + 8, :] for i in range(16)))
    return jnp.concatenate(rows, axis=0)


def contract(a, b, dims):
    return lax.dot_general(a, b, (dims, ((), ())), precision=HI, preferred_element_type=F32)


def dot(a, b):
    return contract(a, b, ((1,), (0,)))


def dot_nt(a, b):
    return contract(a, b, ((1,), (1,)))


def dot_tn(a, b):
    return contract(a, b, ((0,), (0,)))


def inverse_in_place(ref):
    b = HALF // 2

    def step(i, _):
        at = pl.ds(pl.multiple_of(i * b, b), b)
        off = pl.ds(pl.multiple_of((1 - i) * b, b), b)
        pivot = inverse_128(ref[at, at])
        across = dot(pivot, ref[at, off])
        down = ref[off, at]
        ref[off, off] = ref[off, off] - dot(down, across)
        ref[off, at] = -dot(down, pivot)
        ref[at, off] = across
        ref[at, at] = pivot
        return 0

    lax.fori_loop(0, 2, step, 0)


def by_rows(n, body):
    def one(i, _):
        body(pl.ds(pl.multiple_of(i * 128, 128), 128))
        return 0

    lax.fori_loop(0, n // 128, one, 0)


def half_inverse(corner, below, inv_ref, low_ref, below_ref):
    inv_ref[...] = corner
    inverse_in_place(inv_ref)
    below_ref[...] = below

    def some(rows):
        low_ref[rows, :] = dot(below_ref[rows, :], inv_ref[...])

    by_rows(HALF, some)


def whole_inverse(corner, inv, low, below, out_ref, work):
    h = HALF
    work[...] = corner

    def schur(rows):
        work[rows, :] = work[rows, :] - dot_nt(low[rows, :], below[...])

    by_rows(h, schur)
    inverse_in_place(work)

    def lower(rows):
        out_ref[pl.ds(h + rows.start, 128), 0:h] = -dot(work[rows, :], low[...])

    by_rows(h, lower)

    def upper(rows):
        out_ref[rows, 0:h] = inv[rows, :] - dot_tn(low[:, rows], out_ref[h : 2 * h, 0:h])

    by_rows(h, upper)
    out_ref[h : 2 * h, h : 2 * h] = work[...]
    out_ref[0:h, h : 2 * h] = out_ref[h : 2 * h, 0:h].T


def half_one_kernel(mine, other, *outs):
    s = mine[...] + other[...]
    half_inverse(s[0:HALF], s[HALF : 2 * HALF], *outs)


def whole_one_kernel(mine, other, inv, low, below, out, work):
    whole_inverse(mine[...] + other[...], inv, low, below, out, work)


def half_two_kernel(where, mine, other, *outs):
    first = where[0] == 0
    half_inverse(
        jnp.where(first, mine[...], other[...]), jnp.where(first, other[...], mine[...]), *outs
    )


def whole_two_kernel(where, mine, other, inv, low, below, out, work):
    first = where[0] == 0
    corner = jnp.concatenate(
        [jnp.where(first, mine[...], other[...]), jnp.where(first, other[...], mine[...])], axis=0
    )
    whole_inverse(corner, inv, low, below, out, work)


SQUARE = jax.ShapeDtypeStruct((HALF, HALF), F32)
HALF_COST = 16 * 10**9


def pick_rows(idx_ref, start, src, dst, count):
    def eight(g, _):
        base = g * 8
        got = [src[pl.ds(idx_ref[start + base + i], 1), :] for i in range(8)]
        dst[pl.ds(pl.multiple_of(base, 8), 8), :] = jnp.concatenate(got, axis=0)
        return 0

    lax.fori_loop(0, count // 8, eight, 0)


def gather_kernel(idx_ref, a_ref, list_ref, *refs):
    parts, whole, rows = refs[:PARTS], refs[PARTS], refs[PARTS + 1]
    pick_rows(idx_ref, 0, a_ref, rows, EDGE)
    w = whole.shape[0]
    point = lax.broadcasted_iota(jnp.int32, (w, 1), 0) + lax.axis_index("col") * w
    hits = jnp.sum((list_ref[...] == point).astype(F32), axis=1, keepdims=True)
    keep = 1.0 - hits
    for k in range(0, EDGE, 128):
        t = rows[k : k + 128, :].T
        lo = k % HALF
        parts[k // HALF][:, lo : lo + 128] = t
        whole[:, k : k + 128] = t * keep


def select_kernel(start, count, idx_ref, *refs):
    pieces, o_ref, stack = refs[:COLS], refs[COLS], refs[COLS + 1]
    w = pieces[0].shape[0]
    for k, piece in enumerate(pieces):
        stack[k * w : (k + 1) * w, :] = piece[...]
    pick_rows(idx_ref, start, stack, o_ref, count)


def column_of(row, n):
    return jnp.broadcast_to(row, (128, n)).T


def half_of(parity):
    return pl.ds(pl.multiple_of(parity * HALF, HALF), HALF)


def middle_kernel(where, inv, t_own, t_sib, m_ref, mh_ref, ab_ref, d_ref, x_all, y_one):
    parity = where[0]
    x_all[:, half_of(parity)] = t_own[0:IFACE, :]
    x_all[:, half_of(1 - parity)] = t_sib[0:IFACE, :]
    y_one[...] = jnp.where(parity == 1, t_own[IFACE:EDGE, :], t_sib[IFACE:EDGE, :])

    def rows_of_m(rows):
        m_ref[rows, :] = dot(inv[rows, :], x_all[...])

    by_rows(IFACE, rows_of_m)
    mh_ref[...] = m_ref[half_of(parity), :]
    y_zero = jnp.where(parity == 0, t_own[IFACE:EDGE, :], 0.0)
    ab_ref[...] = y_zero

    def rows_of_ab(rows):
        ab_ref[rows, :] = ab_ref[rows, :] - dot_tn(t_own[0:IFACE, rows], m_ref[:, 0:HALF])

    by_rows(HALF, rows_of_ab)
    o = pl.multiple_of(parity * 128, 128)
    part = x_all[:, pl.ds(pl.multiple_of(HALF + parity * 128, 128), 128)]
    d_ref[...] = y_one[pl.ds(o, 128), :] - dot_tn(part, m_ref[:, HALF:IFACE])


def split(v):
    high = v.astype(BF16)
    return high, (v - high.astype(F32)).astype(BF16)


def three(a, b, dims=((1,), (0,))):
    def one(x, y):
        return lax.dot_general(x, y, (dims, ((), ())), preferred_element_type=F32)

    return one(a[0], b[0]) + (one(a[0], b[1]) + one(a[1], b[0]))


def side_kernel(where, inv, m, whole, gt_ref, w_ref):
    m2, inv2 = split(m[...]), split(inv[...])
    mine = half_of(where[0])

    def some(rows):
        pi = split(whole[rows, 0:IFACE])
        w_ref[rows, :] = three(pi, inv2)
        gt_ref[rows, :] = -three(pi, m2)
        gt_ref[rows, mine] = gt_ref[rows, mine] + whole[rows, IFACE:EDGE]

    by_rows(whole.shape[0], some)


def last_kernel(where, inv, m_ref, mz, mz_sib, gt, w1t, a_ref, keep2, keep_col, *refs):
    n_in = 2 * PARTS + 2 * (COLS + 1)
    ins, out = refs[:n_in], refs[n_in]
    edges, both, block, m_far, in_sems, out_sems = refs[n_in + 1 :]
    parity, quad, col = where[0], where[1], where[2]
    w = gt.shape[0]
    child = COLS * w
    copies = [[], [], [], []]

    def load(m, k, src, dst):
        c = pltpu.make_async_copy(src, dst, in_sems.at[m, k])
        c.start()
        copies[m].append(c)

    for m in range(2):
        for k in range(PARTS):
            dst = edges.at[pl.ds(m * child, child), pl.ds(k * HALF, HALF)]
            load(m, k, ins[PARTS * m + k], dst)
    for m in range(2):
        start = (2 + m) * child
        for k in range(COLS + 1):
            piece = ins[2 * PARTS + (COLS + 1) * m + k]
            load(2 + m, k, piece, edges.at[pl.ds(start, piece.shape[0]), :])
            start += piece.shape[0]

    m_far[half_of(parity), :] = mz[...]
    m_far[half_of(1 - parity), :] = mz_sib[...]
    nt = ((1,), (1,))
    inv2, near2, far2 = split(inv[...]), split(m_ref[...]), split(m_far[...])

    def some(rows):
        vt = three(split(gt[rows, :]), inv2)
        vt2 = split(vt)
        u = split((w1t[rows, :] - three(vt2, near2, nt)).T)
        f = split((-three(vt2, far2, nt)).T)
        v = split(vt.T)
        for part in range(2):
            lanes = pl.ds(pl.multiple_of(part * w + rows.start, 128), 128)
            for k in range(4):
                both[k, 0:IFACE, lanes] = (u if k < 2 else f)[part]
            for k in range(2):
                half = v[part][k * HALF : (k + 1) * HALF]
                same = k ^ parity
                both[same, IFACE:EDGE, lanes] = half
                both[same + 2, IFACE:EDGE, lanes] = half

    by_rows(w, some)

    def store(i):
        m, r = i // COLS, i % COLS
        o = (quad ^ m) * child + ((col + r) % COLS) * w
        return pltpu.make_async_copy(
            block.at[i % 2], out.at[pl.ds(pl.multiple_of(o, w), w), :], out_sems.at[i % 2]
        )

    def one(i, _):
        m, r = i // COLS, i % COLS
        for k in range(4):

            @pl.when(i == k * COLS)
            def _():
                for c in copies[k]:
                    c.wait()

        @pl.when(i >= 2)
        def _():
            store(i - 2).wait()

        high, low = split(edges[pl.ds(pl.multiple_of(i * w, w), w), :])
        wide = jnp.dot(high, both[m], preferred_element_type=F32)
        total = wide[:, 0:w] + (
            wide[:, w : 2 * w] + jnp.dot(low, both[m, :, 0:w], preferred_element_type=F32)
        )
        block[i % 2] = -total

        @pl.when(m < 2)
        def _():
            here = pl.ds(pl.multiple_of(((col + r) % COLS) * w, w), w)
            mask = jnp.tile(column_of(keep2[pl.ds(jnp.minimum(m, 1), 1), here], w), (1, w // 128))
            own = jnp.where(m == 0, keep_col[...], 0.0)
            block[i % 2] = (block[i % 2] + a_ref[here, :] * own) * mask

        store(i).start()
        return 0

    lax.fori_loop(0, 4 * COLS, one, 0)
    store(4 * COLS - 2).wait()
    store(4 * COLS - 1).wait()


def swapped(shard, apart):
    n = lax.axis_size("box")
    return lax.ppermute(shard, "box", [(i, i ^ apart) for i in range(n)])


def shifted(shard, by):
    return lax.ppermute(shard, "col", [((i + by) % COLS, i) for i in range(COLS)])


def after(values, *others):
    return lax.optimization_barrier((values, others))[0]


def around(own, forward):
    right, left = shifted(own, 1), shifted(own, -1)
    return (own, right, left), (right if forward == 1 else left)


def farther(near, forward):
    own, right, left = near
    far = shifted(right if forward == 1 else left, forward)
    return own, right, far, left


def farther_both(near, done):
    own, right, left = near
    h = own.shape[0] // 2
    top, bottom = after((right[:h], left[h:]), done)
    far = shifted(top, 1), shifted(bottom, -1)
    return own, right, *far, left


def select(start, count, relative, pieces):
    rows = COLS * pieces[0].shape[0]
    return call(
        functools.partial(select_kernel, start, count),
        (shape(count, HALF), shape(rows, HALF)),
        1,
        COLS,
        3 * 10**9,
        8 * rows * HALF,
    )(relative, *pieces)


def merged(child_maps, iface_one, iface_two):
    a = child_maps[0]
    boundary, w = a.shape
    box, col = lax.axis_index("box"), lax.axis_index("col")
    parity = box % 2
    own_one = iface_one[0]
    group = lax.dynamic_index_in_dim(iface_two, box // 2, 0, keepdims=False)
    own_two = lax.dynamic_slice_in_dim(group, parity * HALF, HALF) - parity * boundary
    points = jnp.concatenate([own_one, own_two])

    *parts, whole = call(
        gather_kernel,
        (shape(w, HALF),) * PARTS + (shape(w, EDGE),),
        1,
        2,
        0,
        4 * boundary * w,
        [pltpu.VMEM((EDGE, w), F32)],
    )(points, a, points[None, :])
    near0, first0 = around(parts[0], 1)
    part0 = farther(near0, 1)
    relative = (points - col * w) % boundary
    where = jnp.stack([parity, box % 4, col]).astype(jnp.int32)
    near1, first1 = around(after(parts[1], first0), -1)
    part1 = farther(near1, -1)
    far = swapped(whole, 2)
    matches = jnp.arange(boundary, dtype=jnp.int32)[None, :] == points[:, None]
    keep = 1.0 - jnp.sum(matches.astype(F32), axis=0)
    keep_col = lax.dynamic_slice_in_dim(keep, col * w, w)[None, :]
    keep2 = jnp.stack([keep, swapped(keep, 1)])

    t0, stack0 = select(0, IFACE, relative, part0)
    t0, t0_sib, where, keep2, keep_col = after(
        (t0, swapped(t0, 1), where, keep2, keep_col), first1
    )
    half = call(half_one_kernel, (SQUARE,) * 3, 0, 2, HALF_COST, 10**6)(t0, t0_sib)

    near2, first2 = around(after(parts[2], first1), 1)
    far2 = shifted(after(parts[2], first1), 2)
    part2 = near2[0], near2[1], far2, near2[2]
    t1, stack1 = select(HALF, HALF, relative, after(part1, half[0]))
    t1, t1_sib = after((t1, swapped(t1, 1)), first2)
    inv_one = call(
        whole_one_kernel, shape(IFACE, IFACE), 0, 5, HALF_COST, 10**6,
        [pltpu.VMEM((HALF, HALF), F32)],
    )(t1, t1_sib, *half)

    nearz, _ = around(after(far, first2), -1)
    t2, stack2 = select(0, EDGE, relative, after(part2, inv_one))
    m, m_half, ab, d = call(
        middle_kernel,
        (shape(IFACE, IFACE), shape(HALF, IFACE), SQUARE, shape(128, HALF)),
        1,
        3,
        5 * 10**9,
        2**22,
        [pltpu.VMEM((IFACE, IFACE), F32), pltpu.VMEM((HALF, HALF), F32)],
    )(where, inv_one, t2, swapped(t2, 1))

    ab_far = swapped(ab, 2)
    gt, w1t = call(
        side_kernel, (shape(w, IFACE),) * 2, 1, 3, 3 * 10**9, 2**22
    )(where, inv_one, m, whole)
    partz = farther_both(nearz, gt)
    ab = ab + after(ab_far, gt)
    ab_sib = swapped(ab, 1)
    d = after(d, ab_far)
    d = d + swapped(d, 2)
    d_sib = swapped(d, 1)
    half = call(half_two_kernel, (SQUARE,) * 3, 1, 2, HALF_COST, 10**6)(where, ab, ab_sib)
    inv_two = call(
        whole_two_kernel, shape(IFACE, IFACE), 1, 5, HALF_COST, 10**6,
        [pltpu.VMEM((HALF, HALF), F32)],
    )(where, d, d_sib, *half)

    m_far = swapped(after(m_half, d), 2)
    stacks = (stack0, stack1, stack2)
    stacks_sib = [swapped(v, 1) for v in stacks]
    partz_sib = [swapped(v, 1) for v in partz]
    out = pl.pallas_call(
        last_kernel,
        name="last",
        out_shape=shape(COLS * boundary, w),
        in_specs=[SMEM] + [VMEM] * 9 + [ANY] * (2 * PARTS + 2 * (COLS + 1)),
        out_specs=ANY,
        scratch_shapes=[
            pltpu.VMEM((4 * boundary, EDGE), F32),
            pltpu.VMEM((4, EDGE, 2 * w), BF16),
            pltpu.VMEM((2, w, w), F32),
            pltpu.VMEM((IFACE, IFACE), F32),
            pltpu.SemaphoreType.DMA((4, COLS + 1)),
            pltpu.SemaphoreType.DMA((2,)),
        ],
        cost_estimate=pl.CostEstimate(flops=10**10, bytes_accessed=3 * 10**7, transcendentals=0),
        compiler_params=pltpu.CompilerParams(vmem_limit_bytes=48 * 2**20),
    )(
        where, inv_two, m, m_far, swapped(m_far, 1), gt, w1t, a, keep2, keep_col,
        *stacks, *stacks_sib, *partz, *partz_sib,
    )
    return out[None]


def solution(mesh):
    return jax.shard_map(
        merged,
        mesh=mesh,
        in_specs=(P("box", None, "col"), P("box", None), P()),
        out_specs=P("box", None, "col"),
        check_vma=False,
    )
```

profile of v0, /device:TPU:1, one launch (start us, length us, event | category | flops | bytes accessed | tf_op | source)
XLA Modules:
  0.0 174.6 jit_solution(11780108924035253631)
XLA Ops:
  0.0 0.8 dynamic-slice_subtract_fusion
  0.8 0.7 pad_add_fusion
  1.5 1.7 copy-done
  3.2 3.7 %shard_map.37 = (f32[384,256]{1,0:T(8,128)S(1)}, f32[384,256]{1,0:T(8,128)}, f32[384,256]{1,0:T(8,128)S(1)}, f32[384,768]{1,0:T(8,128)S(1)}) custom-call(s32[768]{0:T(1024)S(1)} %get-tuple-element.95.idx_ref, f32[1536,384]{1,0:T(8,128)S(1)} %bitcast.8, s32[1,768]{1,0:T(1,128)S(1)} %broadcast_in_dim.11.list_ref), custom_call_target="tpu_custom_call" | custom-call | bytes 2359296 | tf_op jit(solution)/shard_map/pallas_call | solution.py:433
  6.8 3.6 %collective-permute-start = (f32[384,256]{1,0:T(8,128)S(1)}, f32[384,256]{1,0:T(8,128)S(1)}, u32[]{:S(2)}, u32[]{:S(2)}) collective-permute-start(f32[384,256]{1,0:T(8,128)S(1)} %get-tuple-element.50.refs_0_), channel_id=1, source_target_pairs={{1,0},{2,1},{3,2},{0,3},{5,4},{6,5},{7,6},{4,7},{9,8},{10,9},{11,1... | collective-permute-start | bytes 1179656 | tf_op jit(solution)/shard_map/ppermute | solution.py:385
  10.4 7.8 %collective-permute-done.refs_1_ = f32[384,256]{1,0:T(8,128)S(1)} collective-permute-done((f32[384,256]{1,0:T(8,128)S(1)}, f32[384,256]{1,0:T(8,128)S(1)}, u32[]{:S(2)}, u32[]{:S(2)}) %collective-permute-start) | collective-permute-done | bytes 393248 | tf_op jit(solution)/shard_map/ppermute | solution.py:385
  18.2 3.4 %collective-permute-start.1 = (f32[384,256]{1,0:T(8,128)S(1)}, f32[384,256]{1,0:T(8,128)S(1)}, u32[]{:S(2)}, u32[]{:S(2)}) collective-permute-start(f32[384,256]{1,0:T(8,128)S(1)} %collective-permute-done.refs_1_), channel_id=1, source_target_pairs={{1,0},{2,1},{3,2},{0,3},{5,4},{6,5},{7,6},{4,7},{9,8},{10,9},{11,1... | collective-permute-start | bytes 1179656 | tf_op jit(solution)/shard_map/ppermute | solution.py:385
  21.6 0.5 convert_reduce_fusion
  22.2 6.3 %collective-permute-done.1.refs_2_ = f32[384,256]{1,0:T(8,128)S(1)} collective-permute-done((f32[384,256]{1,0:T(8,128)S(1)}, f32[384,256]{1,0:T(8,128)S(1)}, u32[]{:S(2)}, u32[]{:S(2)}) %collective-permute-start.1) | collective-permute-done | bytes 393248 | tf_op jit(solution)/shard_map/ppermute | solution.py:385
  28.5 2.0 %shard_map.38 = (f32[512,256]{1,0:T(8,128)S(1)}, f32[1536,256]{1,0:T(8,128)S(1)}) custom-call(s32[768]{0:T(1024)S(1)} %get-tuple-element.96.idx_ref, f32[384,256]{1,0:T(8,128)S(1)} %get-tuple-element.50.refs_0_, f32[384,256]{1,0:T(8,128)S(1)} %collective-permute-done.refs_1_, f32[384,256]{1,0:T(8,128)S(1)} %collective-permute-done.1.refs_2_, ...), custom_call_target="tpu_custom_call" | custom-call | flops 3000000000 | bytes 3145728 | tf_op jit(solution)/shard_map/pallas_call | solution.py:413
  30.5 2.5 %collective-permute-start.3 = (f32[512,256]{1,0:T(8,128)S(1)}, f32[512,256]{1,0:T(8,128)}, u32[]{:S(2)}, u32[]{:S(2)}) collective-permute-start(f32[512,256]{1,0:T(8,128)S(1)} %get-tuple-element.55.mine), channel_id=1, source_target_pairs={{0,4},{4,0},{8,12},{12,8},{16,20},{20,16},{24,28},{28,24},{32,36},... | collective-permute-start | bytes 1572872 | tf_op jit(solution)/shard_map/ppermute | solution.py:381
  33.0 0.1 collective-permute-start.4
  33.3 1.4 collective-permute-done.4
  34.7 3.5 %collective-permute-start.6 = (f32[384,256]{1,0:T(8,128)}, f32[384,256]{1,0:T(8,128)S(1)}, u32[]{:S(2)}, u32[]{:S(2)}) collective-permute-start(f32[384,256]{1,0:T(8,128)} %get-tuple-element.58.refs_0_), channel_id=1, source_target_pairs={{1,0},{2,1},{3,2},{0,3},{5,4},{6,5},{7,6},{4,7},{9,8},{10,9},{11,1... | collective-permute-start | bytes 1179656 | tf_op jit(solution)/shard_map/ppermute | solution.py:385
  38.3 1.4 collective-permute-start.7
  39.6 12.1 %shard_map.39 = (f32[256,256]{1,0:T(8,128)S(1)}, f32[256,256]{1,0:T(8,128)S(1)}, f32[256,256]{1,0:T(8,128)S(1)}) custom-call(f32[512,256]{1,0:T(8,128)S(1)} %get-tuple-element.55.mine, f32[512,256]{1,0:T(8,128)} %collective-permute-done.3.other), custom_call_target="tpu_custom_call" | custom-call | flops 16000000000 | bytes 1000000 | tf_op jit(solution)/shard_map/pallas_call | solution.py:458
  51.8 1.9 %shard_map.40 = (f32[256,256]{1,0:T(8,128)S(1)}, f32[1536,256]{1,0:T(8,128)S(1)}) custom-call(s32[768]{0:T(1024)S(1)} %get-tuple-element.96.idx_ref, f32[384,256]{1,0:T(8,128)} %get-tuple-element.58.refs_0_, f32[384,256]{1,0:T(8,128)S(1)} %collective-permute-done.6.refs_1_, f32[384,256]{1,0:T(8,128)S(1)} %collective-permute-done.7.refs_2_, ...), custom_call_target="tpu_custom_call" | custom-call | flops 3000000000 | bytes 3145728 | tf_op jit(solution)/shard_map/pallas_call | solution.py:413
  53.7 1.3 collective-permute-start.8
  55.0 1.6 collective-permute-start.22
  56.6 2.2 %collective-permute-start.10 = (f32[384,256]{1,0:T(8,128)S(1)}, f32[384,256]{1,0:T(8,128)S(1)}, u32[]{:S(2)}, u32[]{:S(2)}) collective-permute-start(f32[384,256]{1,0:T(8,128)S(1)} %copy-done.5), channel_id=1, source_target_pairs={{2,0},{3,1},{0,2},{1,3},{6,4},{7,5},{4,6},{5,7},{10,8},{11,9},{8,1... | collective-permute-start | bytes 1179656 | tf_op jit(solution)/shard_map/ppermute | solution.py:385
  58.9 12.6 %shard_map.41.inv = f32[512,512]{1,0:T(8,128)S(1)} custom-call(f32[256,256]{1,0:T(8,128)S(1)} %get-tuple-element.65.mine, f32[256,256]{1,0:T(8,128)S(1)} %collective-permute-done.8.other, f32[256,256]{1,0:T(8,128)S(1)} %get-tuple-element.57.inv, f32[256,256]{1,0:T(8,128)S(1)} %get-tuple-element.67.low, f32[256,256]{1,0:T(8,128)S(1)} %get-tuple-element.68.below), custom_call_target="tpu_custom_call" | custom-call | flops 16000000000 | bytes 1000000 | tf_op jit(solution)/shard_map/pallas_call | solution.py:465
  71.5 4.6 %collective-permute-done.10.refs_2_ = f32[384,256]{1,0:T(8,128)S(1)} collective-permute-done((f32[384,256]{1,0:T(8,128)S(1)}, f32[384,256]{1,0:T(8,128)S(1)}, u32[]{:S(2)}, u32[]{:S(2)}) %collective-permute-start.10) | collective-permute-done | bytes 393248 | tf_op jit(solution)/shard_map/ppermute | solution.py:385
  76.2 2.6 %shard_map.42 = (f32[768,256]{1,0:T(8,128)S(1)}, f32[1536,256]{1,0:T(8,128)S(1)}) custom-call(s32[768]{0:T(1024)S(1)} %get-tuple-element.96.idx_ref, f32[384,256]{1,0:T(8,128)S(1)} %copy-done.5, f32[384,256]{1,0:T(8,128)S(1)} %collective-permute-done.9.refs_1_, f32[384,256]{1,0:T(8,128)S(1)} %collective-permute-done.10.refs_2_, ...), custom_call_target="tpu_custom_call" | custom-call | flops 3000000000 | bytes 3145728 | tf_op jit(solution)/shard_map/pallas_call | solution.py:413
  78.8 1.8 %collective-permute-start.12 = (f32[768,256]{1,0:T(8,128)S(1)}, f32[768,256]{1,0:T(8,128)S(1)}, u32[]{:S(2)}, u32[]{:S(2)}) collective-permute-start(f32[768,256]{1,0:T(8,128)S(1)} %get-tuple-element.73.t_own), channel_id=1, source_target_pairs={{0,4},{4,0},{8,12},{12,8},{16,20},{20,16},{24,28},{28,24},{32,36},... | collective-permute-start | bytes 2359304 | tf_op jit(solution)/shard_map/ppermute | solution.py:381
  80.6 2.1 %collective-permute-done.22.refs_6_ = f32[384,768]{1,0:T(8,128)S(1)} collective-permute-done((f32[384,768]{1,0:T(8,128)S(1)}, f32[384,768]{1,0:T(8,128)S(1)}, u32[]{:S(2)}, u32[]{:S(2)}) %collective-permute-start.22) | collective-permute-done | bytes 1179680 | tf_op jit(solution)/shard_map/ppermute | solution.py:381
  82.8 0.8 collective-permute-start.27
  83.6 2.7 %collective-permute-start.23 = (f32[384,768]{1,0:T(8,128)S(1)}, f32[384,768]{1,0:T(8,128)S(1)}, u32[]{:S(2)}, u32[]{:S(2)}) collective-permute-start(f32[384,768]{1,0:T(8,128)S(1)} %collective-permute-done.22.refs_6_), channel_id=1, source_target_pairs={{1,0},{2,1},{3,2},{0,3},{5,4},{6,5},{7,6},{4,7},{9,8},{10,9},{11,1... | collective-permute-start | bytes 3538952 | tf_op jit(solution)/shard_map/ppermute | solution.py:385
  86.2 4.8 %shard_map.43 = (f32[512,512]{1,0:T(8,128)S(1)}, f32[256,512]{1,0:T(8,128)S(1)}, f32[256,256]{1,0:T(8,128)S(1)}, f32[128,256]{1,0:T(8,128)S(1)}) custom-call(s32[3]{0:T(128)S(1)} %pad_add_fusion.1.where, f32[512,512]{1,0:T(8,128)S(1)} %shard_map.41.inv, f32[768,256]{1,0:T(8,128)S(1)} %get-tuple-element.73.t_own, f32[768,256]{1,0:T(8,128)S(1)} %collective-permute-done.12.t_sib), custom_call_target="tpu_custom_call" | custom-call | flops 5000000000 | bytes 4194304 | tf_op jit(solution)/shard_map/pallas_call | solution.py:472
  91.0 1.5 collective-permute-start.13
  92.6 5.8 %collective-permute-done.13 = f32[256,256]{1,0:T(8,128)S(1)} collective-permute-done((f32[256,256]{1,0:T(8,128)S(1)}, f32[256,256]{1,0:T(8,128)S(1)}, u32[]{:S(2)}, u32[]{:S(2)}) %collective-permute-start.13) | collective-permute-done | bytes 262176 | tf_op jit(solution)/shard_map/ppermute | solution.py:381
  98.4 1.5 collective-permute-start.14
  99.9 2.7 %shard_map.44 = (f32[384,512]{1,0:T(8,128)S(1)}, f32[384,512]{1,0:T(8,128)S(1)}) custom-call(s32[3]{0:T(128)S(1)} %pad_add_fusion.1.where, f32[512,512]{1,0:T(8,128)S(1)} %shard_map.41.inv, f32[512,512]{1,0:T(8,128)S(1)} %get-tuple-element.77.m.m_ref, f32[384,768]{1,0:T(8,128)S(1)} %get-tuple-element.78.whole), custom_call_target="tpu_custom_call" | custom-call | flops 3000000000 | bytes 4194304 | tf_op jit(solution)/shard_map/pallas_call | solution.py:483
  102.6 2.2 %collective-permute-start.16 = (f32[256,256]{1,0:T(8,128)S(1)}, f32[256,256]{1,0:T(8,128)S(1)}, u32[]{:S(2)}, u32[]{:S(2)}) collective-permute-start(f32[256,256]{1,0:T(8,128)S(1)} %add.39.mine), channel_id=1, source_target_pairs={{0,4},{4,0},{8,12},{12,8},{16,20},{20,16},{24,28},{28,24},{32,36},... | collective-permute-start | bytes 786440 | tf_op jit(solution)/shard_map/ppermute | solution.py:381
  105.0 7.3 %collective-permute-done.24.refs_10_ = f32[384,768]{1,0:T(8,128)S(1)} collective-permute-done((f32[384,768]{1,0:T(8,128)S(1)}, f32[384,768]{1,0:T(8,128)S(1)}, u32[]{:S(2)}, u32[]{:S(2)}) %collective-permute-start.24) | collective-permute-done | bytes 1179680 | tf_op jit(solution)/shard_map/ppermute | solution.py:385
  112.3 0.9 collective-permute-start.20
  113.2 0.1 collective-permute-start.21
  113.4 2.7 %collective-permute-start.25 = (f32[192,768]{1,0:T(8,128)S(1)}, f32[192,768]{1,0:T(8,128)S(1)}, u32[]{:S(2)}, u32[]{:S(2)}) collective-permute-start(f32[192,768]{1,0:T(8,128)S(1)} %slice.8), channel_id=1, source_target_pairs={{1,0},{2,1},{3,2},{0,3},{5,4},{6,5},{7,6},{4,7},{9,8},{10,9},{11,1... | collective-permute-start | bytes 1769480 | tf_op jit(solution)/shard_map/ppermute | solution.py:385
  116.1 1.5 collective-permute-start.17
  117.7 11.6 %shard_map.45 = (f32[256,256]{1,0:T(8,128)S(1)}, f32[256,256]{1,0:T(8,128)S(1)}, f32[256,256]{1,0:T(8,128)S(1)}) custom-call(s32[3]{0:T(128)S(1)} %pad_add_fusion.1.where, f32[256,256]{1,0:T(8,128)S(1)} %add.39.mine, f32[256,256]{1,0:T(8,128)S(1)} %collective-permute-done.16.other), custom_call_target="tpu_custom_call" | custom-call | flops 16000000000 | bytes 1000000 | tf_op jit(solution)/shard_map/pallas_call | solution.py:492
  129.3 0.7 collective-permute-start.31
  130.0 0.1 collective-permute-start.28
  130.1 1.8 %collective-permute-done.26.refs_9_ = f32[192,768]{1,0:T(8,128)S(1)} collective-permute-done((f32[192,768]{1,0:T(8,128)S(1)}, f32[192,768]{1,0:T(8,128)S(1)}, u32[]{:S(2)}, u32[]{:S(2)}) %collective-permute-start.26) | collective-permute-done | bytes 589856 | tf_op jit(solution)/shard_map/ppermute | solution.py:385
  131.9 1.2 collective-permute-start.29
  133.2 0.4 collective-permute-start.18
  133.6 13.2 %shard_map.46.inv = f32[512,512]{1,0:T(8,128)S(1)} custom-call(s32[3]{0:T(128)S(1)} %pad_add_fusion.1.where, f32[128,256]{1,0:T(8,128)S(1)} %add.38.mine, f32[128,256]{1,0:T(8,128)S(1)} %collective-permute-done.15.other, f32[256,256]{1,0:T(8,128)S(1)} %get-tuple-element.81.inv, f32[256,256]{1,0:T(8,128)S(1)} %get-tuple-element.82.low, ...), custom_call_target="tpu_custom_call" | custom-call | flops 16000000000 | bytes 1000000 | tf_op jit(solution)/shard_map/pallas_call | solution.py:493
  146.9 0.9 copy-done.14
  147.8 0.4 copy-done.15
  148.2 26.2 %last.1 = f32[6144,384]{1,0:T(8,128)} custom-call(s32[3]{0:T(128)S(1)} %pad_add_fusion.1.where, f32[512,512]{1,0:T(8,128)S(1)} %shard_map.46.inv, f32[512,512]{1,0:T(8,128)} %copy-done.6, f32[256,512]{1,0:T(8,128)S(1)} %collective-permute-done.17.mz, f32[256,512]{1,0:T(8,128)S(1)} %collective-permute-done.18.mz_sib, f32[384,512]{1,0:T(8,128)S(1)} %get-tuple-element.79.gt, ...), custom_call_target="tpu_custom_call" | custom-call | flops 10000000000 | bytes 30000000 | tf_op jit(solution)/shard_map/last/pallas_call | solution.py:502
  (74 shorter events, 0.9 us)
Async XLA Ops:
  1.5 1.7 copy-start
  6.8 23.7 %copy-start.4 = (f32[384,256]{1,0:T(8,128)}, f32[384,256]{1,0:T(8,128)S(1)}, u32[]{:S(2)}) copy-start(f32[384,256]{1,0:T(8,128)S(1)} %get-tuple-element.69.refs_0_) | copy-start | bytes 1179652
  6.8 11.3 %collective-permute-start = (f32[384,256]{1,0:T(8,128)S(1)}, f32[384,256]{1,0:T(8,128)S(1)}, u32[]{:S(2)}, u32[]{:S(2)}) collective-permute-start(f32[384,256]{1,0:T(8,128)S(1)} %get-tuple-element.50.refs_0_), channel_id=1, source_target_pairs={{1,0},{2,1},{3,2},{0,3},{5,4},{6,5},{7,6},{4,7},{9,8},{10,9},{11,1... | collective-permute-start | bytes 1179656 | tf_op jit(solution)/shard_map/ppermute | solution.py:385
  10.4 11.8 %collective-permute-start.2 = (f32[384,256]{1,0:T(8,128)S(1)}, f32[384,256]{1,0:T(8,128)S(1)}, u32[]{:S(2)}, u32[]{:S(2)}) collective-permute-start(f32[384,256]{1,0:T(8,128)S(1)} %get-tuple-element.50.refs_0_), channel_id=1, source_target_pairs={{3,0},{0,1},{1,2},{2,3},{7,4},{4,5},{5,6},{6,7},{11,8},{8,9},{9,10... | collective-permute-start | bytes 1179656 | tf_op jit(solution)/shard_map/ppermute | solution.py:385
  18.2 10.3 %collective-permute-start.1 = (f32[384,256]{1,0:T(8,128)S(1)}, f32[384,256]{1,0:T(8,128)S(1)}, u32[]{:S(2)}, u32[]{:S(2)}) collective-permute-start(f32[384,256]{1,0:T(8,128)S(1)} %collective-permute-done.refs_1_), channel_id=1, source_target_pairs={{1,0},{2,1},{3,2},{0,3},{5,4},{6,5},{7,6},{4,7},{9,8},{10,9},{11,1... | collective-permute-start | bytes 1179656 | tf_op jit(solution)/shard_map/ppermute | solution.py:385
  22.1 16.1 %collective-permute-start.5 = (f32[384,256]{1,0:T(8,128)}, f32[384,256]{1,0:T(8,128)}, u32[]{:S(2)}, u32[]{:S(2)}) collective-permute-start(f32[384,256]{1,0:T(8,128)} %get-tuple-element.58.refs_0_), channel_id=1, source_target_pairs={{3,0},{0,1},{1,2},{2,3},{7,4},{4,5},{5,6},{6,7},{11,8},{8,9},{9,10... | collective-permute-start | bytes 1179656 | tf_op jit(solution)/shard_map/ppermute | solution.py:385
  30.5 50.0 %copy-start.1 = (f32[1536,256]{1,0:T(8,128)}, f32[1536,256]{1,0:T(8,128)S(1)}, u32[]{:S(2)}) copy-start(f32[1536,256]{1,0:T(8,128)S(1)} %get-tuple-element.89.refs_0_) | copy-start | bytes 4718596
  30.5 9.1 %collective-permute-start.3 = (f32[512,256]{1,0:T(8,128)S(1)}, f32[512,256]{1,0:T(8,128)}, u32[]{:S(2)}, u32[]{:S(2)}) collective-permute-start(f32[512,256]{1,0:T(8,128)S(1)} %get-tuple-element.55.mine), channel_id=1, source_target_pairs={{0,4},{4,0},{8,12},{12,8},{16,20},{20,16},{24,28},{28,24},{32,36},... | collective-permute-start | bytes 1572872 | tf_op jit(solution)/shard_map/ppermute | solution.py:381
  33.0 1.7 collective-permute-start.4
  34.7 17.1 %collective-permute-start.6 = (f32[384,256]{1,0:T(8,128)}, f32[384,256]{1,0:T(8,128)S(1)}, u32[]{:S(2)}, u32[]{:S(2)}) collective-permute-start(f32[384,256]{1,0:T(8,128)} %get-tuple-element.58.refs_0_), channel_id=1, source_target_pairs={{1,0},{2,1},{3,2},{0,3},{5,4},{6,5},{7,6},{4,7},{9,8},{10,9},{11,1... | collective-permute-start | bytes 1179656 | tf_op jit(solution)/shard_map/ppermute | solution.py:385
  38.2 20.7 %collective-permute-start.9 = (f32[384,256]{1,0:T(8,128)}, f32[384,256]{1,0:T(8,128)S(1)}, u32[]{:S(2)}, u32[]{:S(2)}) collective-permute-start(f32[384,256]{1,0:T(8,128)} %copy-done.4), channel_id=1, source_target_pairs={{1,0},{2,1},{3,2},{0,3},{5,4},{6,5},{7,6},{4,7},{9,8},{10,9},{11,1... | collective-permute-start | bytes 1179656 | tf_op jit(solution)/shard_map/ppermute | solution.py:385
  38.3 13.5 %collective-permute-start.7 = (f32[384,256]{1,0:T(8,128)}, f32[384,256]{1,0:T(8,128)S(1)}, u32[]{:S(2)}, u32[]{:S(2)}) collective-permute-start(f32[384,256]{1,0:T(8,128)} %collective-permute-done.5.refs_3_), channel_id=1, source_target_pairs={{3,0},{0,1},{1,2},{2,3},{7,4},{4,5},{5,6},{6,7},{11,8},{8,9},{9,10... | collective-permute-start | bytes 1179656 | tf_op jit(solution)/shard_map/ppermute | solution.py:385
  51.7 4.9 %copy-start.5 = (f32[384,256]{1,0:T(8,128)S(1)}, f32[384,256]{1,0:T(8,128)}, u32[]{:S(2)}) copy-start(f32[384,256]{1,0:T(8,128)} %copy-done.4) | copy-start | bytes 1179652
  53.7 58.6 %copy-start.2 = (f32[1536,256]{1,0:T(8,128)}, f32[1536,256]{1,0:T(8,128)S(1)}, u32[]{:S(2)}) copy-start(f32[1536,256]{1,0:T(8,128)S(1)} %get-tuple-element.90.refs_1_) | copy-start | bytes 4718596
  53.7 5.2 %collective-permute-start.8 = (f32[256,256]{1,0:T(8,128)S(1)}, f32[256,256]{1,0:T(8,128)S(1)}, u32[]{:S(2)}, u32[]{:S(2)}) collective-permute-start(f32[256,256]{1,0:T(8,128)S(1)} %get-tuple-element.65.mine), channel_id=1, source_target_pairs={{0,4},{4,0},{8,12},{12,8},{16,20},{20,16},{24,28},{28,24},{32,36},... | collective-permute-start | bytes 786440 | tf_op jit(solution)/shard_map/ppermute | solution.py:381
  55.0 27.8 %collective-permute-start.22 = (f32[384,768]{1,0:T(8,128)S(1)}, f32[384,768]{1,0:T(8,128)S(1)}, u32[]{:S(2)}, u32[]{:S(2)}) collective-permute-start(f32[384,768]{1,0:T(8,128)S(1)} %get-tuple-element.78.whole), channel_id=1, source_target_pairs={{0,8},{4,12},{8,0},{12,4},{16,24},{20,28},{24,16},{28,20},{32,40},... | collective-permute-start | bytes 3538952 | tf_op jit(solution)/shard_map/ppermute | solution.py:381
  56.6 14.9 %collective-permute-start.11 = (f32[384,256]{1,0:T(8,128)S(1)}, f32[384,256]{1,0:T(8,128)S(1)}, u32[]{:S(2)}, u32[]{:S(2)}) collective-permute-start(f32[384,256]{1,0:T(8,128)S(1)} %copy-done.5), channel_id=1, source_target_pairs={{3,0},{0,1},{1,2},{2,3},{7,4},{4,5},{5,6},{6,7},{11,8},{8,9},{9,10... | collective-permute-start | bytes 1179656 | tf_op jit(solution)/shard_map/ppermute | solution.py:385
  56.6 19.5 %collective-permute-start.10 = (f32[384,256]{1,0:T(8,128)S(1)}, f32[384,256]{1,0:T(8,128)S(1)}, u32[]{:S(2)}, u32[]{:S(2)}) collective-permute-start(f32[384,256]{1,0:T(8,128)S(1)} %copy-done.5), channel_id=1, source_target_pairs={{2,0},{3,1},{0,2},{1,3},{6,4},{7,5},{4,6},{5,7},{10,8},{11,9},{8,1... | collective-permute-start | bytes 1179656 | tf_op jit(solution)/shard_map/ppermute | solution.py:385
  78.8 34.4 %copy-start.3 = (f32[1536,256]{1,0:T(8,128)}, f32[1536,256]{1,0:T(8,128)S(1)}, u32[]{:S(2)}) copy-start(f32[1536,256]{1,0:T(8,128)S(1)} %get-tuple-element.91.refs_2_) | copy-start | bytes 4718596
  78.8 7.5 %collective-permute-start.12 = (f32[768,256]{1,0:T(8,128)S(1)}, f32[768,256]{1,0:T(8,128)S(1)}, u32[]{:S(2)}, u32[]{:S(2)}) collective-permute-start(f32[768,256]{1,0:T(8,128)S(1)} %get-tuple-element.73.t_own), channel_id=1, source_target_pairs={{0,4},{4,0},{8,12},{12,8},{16,20},{20,16},{24,28},{28,24},{32,36},... | collective-permute-start | bytes 2359304 | tf_op jit(solution)/shard_map/ppermute | solution.py:381
  80.5 32.9 %collective-permute-start.19 = (f32[1536,256]{1,0:T(8,128)S(1)}, f32[1536,256]{1,0:T(8,128)S(1)}, u32[]{:S(2)}, u32[]{:S(2)}) collective-permute-start(f32[1536,256]{1,0:T(8,128)S(1)} %get-tuple-element.89.refs_0_), channel_id=1, source_target_pairs={{0,4},{4,0},{8,12},{12,8},{16,20},{20,16},{24,28},{28,24},{32,36},... | collective-permute-start | bytes 4718600 | tf_op jit(solution)/shard_map/ppermute | solution.py:381
  82.8 8.2 %copy-start.12 = (f32[384,768]{1,0:T(8,128)}, f32[384,768]{1,0:T(8,128)S(1)}, u32[]{:S(2)}) copy-start(f32[384,768]{1,0:T(8,128)S(1)} %collective-permute-done.22.refs_6_) | copy-start | bytes 3538948
  82.8 22.1 %collective-permute-start.27 = (f32[384,768]{1,0:T(8,128)S(1)}, f32[384,768]{1,0:T(8,128)S(1)}, u32[]{:S(2)}, u32[]{:S(2)}) collective-permute-start(f32[384,768]{1,0:T(8,128)S(1)} %collective-permute-done.22.refs_6_), channel_id=1, source_target_pairs={{0,4},{4,0},{8,12},{12,8},{16,20},{20,16},{24,28},{28,24},{32,36},... | collective-permute-start | bytes 3538952 | tf_op jit(solution)/shard_map/ppermute | solution.py:381
  83.6 28.7 %collective-permute-start.24 = (f32[384,768]{1,0:T(8,128)S(1)}, f32[384,768]{1,0:T(8,128)S(1)}, u32[]{:S(2)}, u32[]{:S(2)}) collective-permute-start(f32[384,768]{1,0:T(8,128)S(1)} %collective-permute-done.22.refs_6_), channel_id=1, source_target_pairs={{3,0},{0,1},{1,2},{2,3},{7,4},{4,5},{5,6},{6,7},{11,8},{8,9},{9,10... | collective-permute-start | bytes 3538952 | tf_op jit(solution)/shard_map/ppermute | solution.py:385
  83.6 29.6 %collective-permute-start.23 = (f32[384,768]{1,0:T(8,128)S(1)}, f32[384,768]{1,0:T(8,128)S(1)}, u32[]{:S(2)}, u32[]{:S(2)}) collective-permute-start(f32[384,768]{1,0:T(8,128)S(1)} %collective-permute-done.22.refs_6_), channel_id=1, source_target_pairs={{1,0},{2,1},{3,2},{0,3},{5,4},{6,5},{7,6},{4,7},{9,8},{10,9},{11,1... | collective-permute-start | bytes 3538952 | tf_op jit(solution)/shard_map/ppermute | solution.py:385
  91.0 11.6 %copy-start.6 = (f32[512,512]{1,0:T(8,128)}, f32[512,512]{1,0:T(8,128)S(1)}, u32[]{:S(2)}) copy-start(f32[512,512]{1,0:T(8,128)S(1)} %get-tuple-element.77.m.m_ref) | copy-start | bytes 3145732
  91.0 7.4 %collective-permute-start.13 = (f32[256,256]{1,0:T(8,128)S(1)}, f32[256,256]{1,0:T(8,128)S(1)}, u32[]{:S(2)}, u32[]{:S(2)}) collective-permute-start(f32[256,256]{1,0:T(8,128)S(1)} %get-tuple-element.75), channel_id=1, source_target_pairs={{0,8},{4,12},{8,0},{12,4},{16,24},{20,28},{24,16},{28,20},{32,40},... | collective-permute-start | bytes 786440 | tf_op jit(solution)/shard_map/ppermute | solution.py:381
  98.4 4.2 %collective-permute-start.14 = (f32[128,256]{1,0:T(8,128)S(1)}, f32[128,256]{1,0:T(8,128)S(1)}, u32[]{:S(2)}, u32[]{:S(2)}) collective-permute-start(f32[128,256]{1,0:T(8,128)S(1)} %get-tuple-element.76), channel_id=1, source_target_pairs={{0,8},{4,12},{8,0},{12,4},{16,24},{20,28},{24,16},{28,20},{32,40},... | collective-permute-start | bytes 393224 | tf_op jit(solution)/shard_map/ppermute | solution.py:381
  102.6 13.5 %collective-permute-start.16 = (f32[256,256]{1,0:T(8,128)S(1)}, f32[256,256]{1,0:T(8,128)S(1)}, u32[]{:S(2)}, u32[]{:S(2)}) collective-permute-start(f32[256,256]{1,0:T(8,128)S(1)} %add.39.mine), channel_id=1, source_target_pairs={{0,4},{4,0},{8,12},{12,8},{16,20},{20,16},{24,28},{28,24},{32,36},... | collective-permute-start | bytes 786440 | tf_op jit(solution)/shard_map/ppermute | solution.py:381
  104.9 8.3 %copy-start.13 = (f32[384,768]{1,0:T(8,128)}, f32[384,768]{1,0:T(8,128)S(1)}, u32[]{:S(2)}) copy-start(f32[384,768]{1,0:T(8,128)S(1)} %collective-permute-done.27.refs_11_) | copy-start | bytes 3538948
  104.9 11.3 %collective-permute-start.15 = (f32[128,256]{1,0:T(8,128)S(1)}, f32[128,256]{1,0:T(8,128)S(1)}, u32[]{:S(2)}, u32[]{:S(2)}) collective-permute-start(f32[128,256]{1,0:T(8,128)S(1)} %add.38.mine), channel_id=1, source_target_pairs={{0,4},{4,0},{8,12},{12,8},{16,20},{20,16},{24,28},{28,24},{32,36},... | collective-permute-start | bytes 393224 | tf_op jit(solution)/shard_map/ppermute | solution.py:381
  112.3 17.0 %copy-start.7 = (f32[384,768]{1,0:T(8,128)}, f32[384,768]{1,0:T(8,128)S(1)}, u32[]{:S(2)}) copy-start(f32[384,768]{1,0:T(8,128)S(1)} %collective-permute-done.24.refs_10_) | copy-start | bytes 3538948
  112.3 17.0 %collective-permute-start.20 = (f32[1536,256]{1,0:T(8,128)S(1)}, f32[1536,256]{1,0:T(8,128)S(1)}, u32[]{:S(2)}, u32[]{:S(2)}) collective-permute-start(f32[1536,256]{1,0:T(8,128)S(1)} %get-tuple-element.90.refs_1_), channel_id=1, source_target_pairs={{0,4},{4,0},{8,12},{12,8},{16,20},{20,16},{24,28},{28,24},{32,36},... | collective-permute-start | bytes 4718600 | tf_op jit(solution)/shard_map/ppermute | solution.py:381
  113.2 16.8 %copy-start.8 = (f32[384,768]{1,0:T(8,128)}, f32[384,768]{1,0:T(8,128)S(1)}, u32[]{:S(2)}) copy-start(f32[384,768]{1,0:T(8,128)S(1)} %collective-permute-done.23.refs_7_) | copy-start | bytes 3538948
  113.2 19.9 %collective-permute-start.21 = (f32[1536,256]{1,0:T(8,128)S(1)}, f32[1536,256]{1,0:T(8,128)S(1)}, u32[]{:S(2)}, u32[]{:S(2)}) collective-permute-start(f32[1536,256]{1,0:T(8,128)S(1)} %get-tuple-element.91.refs_2_), channel_id=1, source_target_pairs={{0,4},{4,0},{8,12},{12,8},{16,20},{20,16},{24,28},{28,24},{32,36},... | collective-permute-start | bytes 4718600 | tf_op jit(solution)/shard_map/ppermute | solution.py:381
  113.4 2.7 %copy-start.9 = (f32[1536,256]{1,0:T(8,128)}, f32[1536,256]{1,0:T(8,128)S(1)}, u32[]{:S(2)}) copy-start(f32[1536,256]{1,0:T(8,128)S(1)} %collective-permute-done.19.refs_3_) | copy-start | bytes 4718596
  113.4 16.6 %collective-permute-start.25 = (f32[192,768]{1,0:T(8,128)S(1)}, f32[192,768]{1,0:T(8,128)S(1)}, u32[]{:S(2)}, u32[]{:S(2)}) collective-permute-start(f32[192,768]{1,0:T(8,128)S(1)} %slice.8), channel_id=1, source_target_pairs={{1,0},{2,1},{3,2},{0,3},{5,4},{6,5},{7,6},{4,7},{9,8},{10,9},{11,1... | collective-permute-start | bytes 1769480 | tf_op jit(solution)/shard_map/ppermute | solution.py:385
  116.1 15.8 %collective-permute-start.26 = (f32[192,768]{1,0:T(8,128)S(1)}, f32[192,768]{1,0:T(8,128)S(1)}, u32[]{:S(2)}, u32[]{:S(2)}) collective-permute-start(f32[192,768]{1,0:T(8,128)S(1)} %slice.9), channel_id=1, source_target_pairs={{3,0},{0,1},{1,2},{2,3},{7,4},{4,5},{5,6},{6,7},{11,8},{8,9},{9,10... | collective-permute-start | bytes 1769480 | tf_op jit(solution)/shard_map/ppermute | solution.py:385
  116.1 17.0 %collective-permute-start.17 = (f32[256,512]{1,0:T(8,128)S(1)}, f32[256,512]{1,0:T(8,128)S(1)}, u32[]{:S(2)}, u32[]{:S(2)}) collective-permute-start(f32[256,512]{1,0:T(8,128)S(1)} %get-tuple-element.85), channel_id=1, source_target_pairs={{0,8},{4,12},{8,0},{12,4},{16,24},{20,28},{24,16},{28,20},{32,40},... | collective-permute-start | bytes 1572872 | tf_op jit(solution)/shard_map/ppermute | solution.py:381
  129.3 17.5 %copy-start.10 = (f32[1536,256]{1,0:T(8,128)}, f32[1536,256]{1,0:T(8,128)S(1)}, u32[]{:S(2)}) copy-start(f32[1536,256]{1,0:T(8,128)S(1)} %collective-permute-done.20.refs_4_) | copy-start | bytes 4718596
  129.3 17.5 %collective-permute-start.31 = (f32[384,768]{1,0:T(8,128)S(1)}, f32[384,768]{1,0:T(8,128)S(1)}, u32[]{:S(2)}, u32[]{:S(2)}) collective-permute-start(f32[384,768]{1,0:T(8,128)S(1)} %collective-permute-done.24.refs_10_), channel_id=1, source_target_pairs={{0,4},{4,0},{8,12},{12,8},{16,20},{20,16},{24,28},{28,24},{32,36},... | collective-permute-start | bytes 3538952 | tf_op jit(solution)/shard_map/ppermute | solution.py:381
  130.0 16.9 %collective-permute-start.28 = (f32[384,768]{1,0:T(8,128)S(1)}, f32[384,768]{1,0:T(8,128)S(1)}, u32[]{:S(2)}, u32[]{:S(2)}) collective-permute-start(f32[384,768]{1,0:T(8,128)S(1)} %collective-permute-done.23.refs_7_), channel_id=1, source_target_pairs={{0,4},{4,0},{8,12},{12,8},{16,20},{20,16},{24,28},{28,24},{32,36},... | collective-permute-start | bytes 3538952 | tf_op jit(solution)/shard_map/ppermute | solution.py:381
  131.9 14.9 %collective-permute-start.29 = (f32[192,768]{1,0:T(8,128)S(1)}, f32[192,768]{1,0:T(8,128)S(1)}, u32[]{:S(2)}, u32[]{:S(2)}) collective-permute-start(f32[192,768]{1,0:T(8,128)S(1)} %collective-permute-done.25.refs_8_), channel_id=1, source_target_pairs={{0,4},{4,0},{8,12},{12,8},{16,20},{20,16},{24,28},{28,24},{32,36},... | collective-permute-start | bytes 1769480 | tf_op jit(solution)/shard_map/ppermute | solution.py:381
  133.1 13.7 %copy-start.11 = (f32[1536,256]{1,0:T(8,128)}, f32[1536,256]{1,0:T(8,128)S(1)}, u32[]{:S(2)}) copy-start(f32[1536,256]{1,0:T(8,128)S(1)} %collective-permute-done.21.refs_5_) | copy-start | bytes 4718596
  133.1 13.7 %collective-permute-start.30 = (f32[192,768]{1,0:T(8,128)S(1)}, f32[192,768]{1,0:T(8,128)S(1)}, u32[]{:S(2)}, u32[]{:S(2)}) collective-permute-start(f32[192,768]{1,0:T(8,128)S(1)} %collective-permute-done.26.refs_9_), channel_id=1, source_target_pairs={{0,4},{4,0},{8,12},{12,8},{16,20},{20,16},{24,28},{28,24},{32,36},... | collective-permute-start | bytes 1769480 | tf_op jit(solution)/shard_map/ppermute | solution.py:381
  133.2 13.7 %collective-permute-start.18 = (f32[256,512]{1,0:T(8,128)S(1)}, f32[256,512]{1,0:T(8,128)S(1)}, u32[]{:S(2)}, u32[]{:S(2)}) collective-permute-start(f32[256,512]{1,0:T(8,128)S(1)} %collective-permute-done.17.mz), channel_id=1, source_target_pairs={{0,4},{4,0},{8,12},{12,8},{16,20},{20,16},{24,28},{28,24},{32,36},... | collective-permute-start | bytes 1572872 | tf_op jit(solution)/shard_map/ppermute | solution.py:381
  146.8 1.0 copy-start.14
  146.8 1.4 copy-start.15
where the time goes:
time: 175 us
  Pallas kernels  93.2 us (53%)
  starting transfers between devices  38 us (22%)
  waiting for transfers between devices  37.3 us (21%)
  local copies, waits for them, and re-layouts  3.24 us (2%)
  other arithmetic  2.15 us (1%)
    ppermute x13, waiting for transfers between devices, shifted(): lax.ppermute(shard, 'col', [((i + by) % COLS, i) for i in range(COLS)])  27.9 us
    pallas_call x1, Pallas kernels, merged(): pl.pallas_call(last_kernel, name='last', out_shape=shape(COLS * boundary,...  26.2 us
    ppermute x13, starting transfers between devices, shifted(): lax.ppermute(shard, 'col', [((i + by) % COLS, i) for i in range(COLS)])  19.6 us
    ppermute x19, starting transfers between devices, swapped(): return lax.ppermute(shard, 'box', [(i, i ^ apart) for i in range(n)])  18.4 us
    pallas_call x1, Pallas kernels, merged(): call(whole_two_kernel, shape(IFACE, IFACE), 1, 5, HALF_COST, 10 ** 6, [pl...  13.2 us
    pallas_call x1, Pallas kernels, merged(): call(whole_one_kernel, shape(IFACE, IFACE), 0, 5, HALF_COST, 10 ** 6, [pl...  12.6 us
    pallas_call x1, Pallas kernels, merged(): call(half_one_kernel, (SQUARE,) * 3, 0, 2, HALF_COST, 10 ** 6)(t0, t0_sib)  12.1 us
    pallas_call x1, Pallas kernels, merged(): call(half_two_kernel, (SQUARE,) * 3, 1, 2, HALF_COST, 10 ** 6)  11.6 us
  transfers between devices with their start and end apart: 32, of which 8 were waited for; matrix products, arithmetic and copies ran while one was open for 0% of the time, Pallas kernels for 36%

commit v1 on v0

--- a/solution.py
+++ b/solution.py
@@ -17,6 +17,7 @@
 PARTS = EDGE // HALF
 
 
+TOGETHER = 2
 PER = 4
 
 VMEM = pl.BlockSpec(memory_space=pltpu.VMEM)
@@ -334,27 +335,31 @@
 
     by_rows(w, some)
 
-    def store(i):
-        m, r = i // COLS, i % COLS
+    def store(i, j):
+        m, r = i * TOGETHER // COLS, i * TOGETHER % COLS + j
         o = (quad ^ m) * child + ((col + r) % COLS) * w
         return pltpu.make_async_copy(
-            block.at[i % 2], out.at[pl.ds(pl.multiple_of(o, w), w), :], out_sems.at[i % 2]
+            block.at[i % 2, pl.ds(j * w, w), :],
+            out.at[pl.ds(pl.multiple_of(o, w), w), :],
+            out_sems.at[i % 2, j],
         )
 
     def one(i, _):
-        m, r = i // COLS, i % COLS
+        m, r = i * TOGETHER // COLS, i * TOGETHER % COLS
         for k in range(4):
 
-            @pl.when(i == k * COLS)
+            @pl.when(i == k * COLS // TOGETHER)
             def _():
                 for c in copies[k]:
                     c.wait()
 
         @pl.when(i >= 2)
         def _():
-            store(i - 2).wait()
-
-        high, low = split(edges[pl.ds(pl.multiple_of(i * w, w), w), :])
+            for j in range(TOGETHER):
+                store(i - 2, j).wait()
+
+        size = TOGETHER * w
+        high, low = split(edges[pl.ds(pl.multiple_of(i * size, size), size), :])
         wide = jnp.dot(high, both[m], preferred_element_type=F32)
         total = wide[:, 0:w] + (
             wide[:, w : 2 * w] + jnp.dot(low, both[m, :, 0:w], preferred_element_type=F32)
@@ -363,17 +368,24 @@
 
         @pl.when(m < 2)
         def _():
-            here = pl.ds(pl.multiple_of(((col + r) % COLS) * w, w), w)
-            mask = jnp.tile(column_of(keep2[pl.ds(jnp.minimum(m, 1), 1), here], w), (1, w // 128))
             own = jnp.where(m == 0, keep_col[...], 0.0)
-            block[i % 2] = (block[i % 2] + a_ref[here, :] * own) * mask
-
-        store(i).start()
+            for j in range(TOGETHER):
+                here = pl.ds(pl.multiple_of(((col + r + j) % COLS) * w, w), w)
+                rows = slice(j * w, (j + 1) * w)
+                mask = column_of(keep2[pl.ds(jnp.minimum(m, 1), 1), here], w)
+                block[i % 2, rows] = (block[i % 2, rows] + a_ref[here, :] * own) * jnp.tile(
+                    mask, (1, w // 128)
+                )
+
+        for j in range(TOGETHER):
+            store(i, j).start()
         return 0
 
-    lax.fori_loop(0, 4 * COLS, one, 0)
-    store(4 * COLS - 2).wait()
-    store(4 * COLS - 1).wait()
+    steps = 4 * COLS // TOGETHER
+    lax.fori_loop(0, steps, one, 0)
+    for j in range(TOGETHER):
+        store(steps - 2, j).wait()
+        store(steps - 1, j).wait()
 
 
 def swapped(shard, apart):
@@ -457,9 +469,10 @@
     )
     half = call(half_one_kernel, (SQUARE,) * 3, 0, 2, HALF_COST, 10**6)(t0, t0_sib)
 
-    near2, first2 = around(after(parts[2], first1), 1)
-    far2 = shifted(after(parts[2], first1), 2)
-    part2 = near2[0], near2[1], far2, near2[2]
+    right2 = shifted(after(parts[2], first0), 1)
+    own2 = after(parts[2], first1)
+    left2, far2 = shifted(own2, -1), shifted(own2, 2)
+    part2, first2 = (parts[2], right2, far2, left2), right2
     t1, stack1 = select(HALF, HALF, relative, after(part1, half[0]))
     t1, t1_sib = after((t1, swapped(t1, 1)), first2)
     inv_one = call(
@@ -508,10 +521,10 @@
         scratch_shapes=[
             pltpu.VMEM((4 * boundary, EDGE), F32),
             pltpu.VMEM((4, EDGE, 2 * w), BF16),
-            pltpu.VMEM((2, w, w), F32),
+            pltpu.VMEM((2, TOGETHER * w, w), F32),
             pltpu.VMEM((IFACE, IFACE), F32),
             pltpu.SemaphoreType.DMA((4, COLS + 1)),
-            pltpu.SemaphoreType.DMA((2,)),
+            pltpu.SemaphoreType.DMA((2, TOGETHER)),
         ],
         cost_estimate=pl.CostEstimate(flops=10**10, bytes_accessed=3 * 10**7, transcendentals=0),
         compiler_params=pltpu.CompilerParams(vmem_limit_bytes=48 * 2**20),

time: 175 us -> 173 us (0.989)
  transfers between devices with their start and end apart: 32 -> 32, of which waited for: 8 -> 8; matrix products, arithmetic and copies ran while one was open for 0% -> 0% of each run, Pallas kernels for 36% -> 37%
where the time goes in v1:
time: 173 us
  Pallas kernels  91.6 us (53%)
  starting transfers between devices  38 us (22%)
  waiting for transfers between devices  37.3 us (22%)
  local copies, waits for them, and re-layouts  3.24 us (2%)
  other arithmetic  2.15 us (1%)
    ppermute x13, waiting for transfers between devices, shifted(): lax.ppermute(shard, 'col', [((i + by) % COLS, i) for i in range(COLS)])  27.9 us
    pallas_call x1, Pallas kernels, merged(): pl.pallas_call(last_kernel, name='last', out_shape=shape(COLS * boundary,...  24.5 us
    ppermute x13, starting transfers between devices, shifted(): lax.ppermute(shard, 'col', [((i + by) % COLS, i) for i in range(COLS)])  19.6 us
    ppermute x19, starting transfers between devices, swapped(): return lax.ppermute(shard, 'box', [(i, i ^ apart) for i in range(n)])  18.4 us
    pallas_call x1, Pallas kernels, merged(): call(whole_two_kernel, shape(IFACE, IFACE), 1, 5, HALF_COST, 10 ** 6, [pl...  13.2 us
    pallas_call x1, Pallas kernels, merged(): call(whole_one_kernel, shape(IFACE, IFACE), 0, 5, HALF_COST, 10 ** 6, [pl...  12.6 us
    pallas_call x1, Pallas kernels, merged(): call(half_one_kernel, (SQUARE,) * 3, 0, 2, HALF_COST, 10 ** 6)(t0, t0_sib)  12.1 us
    pallas_call x1, Pallas kernels, merged(): call(half_two_kernel, (SQUARE,) * 3, 1, 2, HALF_COST, 10 ** 6)  11.6 us
  transfers between devices with their start and end apart: 32, of which 8 were waited for; matrix products, arithmetic and copies ran while one was open for 0% of the time, Pallas kernels for 37%

profile of v1, /device:TPU:1, one launch (start us, length us, event | category | flops | bytes accessed | tf_op | source)
XLA Modules:
  0.0 172.9 jit_solution(9453624259388259814)
XLA Ops:
  0.0 0.8 dynamic-slice_subtract_fusion
  0.8 0.7 pad_add_fusion
  1.5 1.7 copy-done
  3.2 3.7 %shard_map.37 = (f32[384,256]{1,0:T(8,128)S(1)}, f32[384,256]{1,0:T(8,128)}, f32[384,256]{1,0:T(8,128)S(1)}, f32[384,768]{1,0:T(8,128)S(1)}) custom-call(s32[768]{0:T(1024)S(1)} %get-tuple-element.97.idx_ref, f32[1536,384]{1,0:T(8,128)S(1)} %bitcast.8, s32[1,768]{1,0:T(1,128)S(1)} %broadcast_in_dim.11.list_ref), custom_call_target="tpu_custom_call" | custom-call | bytes 2359296 | tf_op jit(solution)/shard_map/pallas_call | solution.py:445
  6.8 3.6 %collective-permute-start = (f32[384,256]{1,0:T(8,128)S(1)}, f32[384,256]{1,0:T(8,128)S(1)}, u32[]{:S(2)}, u32[]{:S(2)}) collective-permute-start(f32[384,256]{1,0:T(8,128)S(1)} %get-tuple-element.51.refs_0_), channel_id=1, source_target_pairs={{1,0},{2,1},{3,2},{0,3},{5,4},{6,5},{7,6},{4,7},{9,8},{10,9},{11,1... | collective-permute-start | bytes 1179656 | tf_op jit(solution)/shard_map/ppermute | solution.py:397
  10.4 7.8 %collective-permute-done.refs_1_ = f32[384,256]{1,0:T(8,128)S(1)} collective-permute-done((f32[384,256]{1,0:T(8,128)S(1)}, f32[384,256]{1,0:T(8,128)S(1)}, u32[]{:S(2)}, u32[]{:S(2)}) %collective-permute-start) | collective-permute-done | bytes 393248 | tf_op jit(solution)/shard_map/ppermute | solution.py:397
  18.2 3.4 %collective-permute-start.1 = (f32[384,256]{1,0:T(8,128)S(1)}, f32[384,256]{1,0:T(8,128)S(1)}, u32[]{:S(2)}, u32[]{:S(2)}) collective-permute-start(f32[384,256]{1,0:T(8,128)S(1)} %collective-permute-done.refs_1_), channel_id=1, source_target_pairs={{1,0},{2,1},{3,2},{0,3},{5,4},{6,5},{7,6},{4,7},{9,8},{10,9},{11,1... | collective-permute-start | bytes 1179656 | tf_op jit(solution)/shard_map/ppermute | solution.py:397
  21.6 0.5 convert_reduce_fusion
  22.2 6.3 %collective-permute-done.1.refs_2_ = f32[384,256]{1,0:T(8,128)S(1)} collective-permute-done((f32[384,256]{1,0:T(8,128)S(1)}, f32[384,256]{1,0:T(8,128)S(1)}, u32[]{:S(2)}, u32[]{:S(2)}) %collective-permute-start.1) | collective-permute-done | bytes 393248 | tf_op jit(solution)/shard_map/ppermute | solution.py:397
  28.5 2.0 %shard_map.38 = (f32[512,256]{1,0:T(8,128)S(1)}, f32[1536,256]{1,0:T(8,128)S(1)}) custom-call(s32[768]{0:T(1024)S(1)} %get-tuple-element.98.idx_ref, f32[384,256]{1,0:T(8,128)S(1)} %get-tuple-element.51.refs_0_, f32[384,256]{1,0:T(8,128)S(1)} %collective-permute-done.refs_1_, f32[384,256]{1,0:T(8,128)S(1)} %collective-permute-done.1.refs_2_, ...), custom_call_target="tpu_custom_call" | custom-call | flops 3000000000 | bytes 3145728 | tf_op jit(solution)/shard_map/pallas_call | solution.py:425
  30.5 2.5 %collective-permute-start.3 = (f32[512,256]{1,0:T(8,128)S(1)}, f32[512,256]{1,0:T(8,128)}, u32[]{:S(2)}, u32[]{:S(2)}) collective-permute-start(f32[512,256]{1,0:T(8,128)S(1)} %get-tuple-element.56.mine), channel_id=1, source_target_pairs={{0,4},{4,0},{8,12},{12,8},{16,20},{20,16},{24,28},{28,24},{32,36},... | collective-permute-start | bytes 1572872 | tf_op jit(solution)/shard_map/ppermute | solution.py:393
  33.0 0.1 collective-permute-start.4
  33.3 1.4 collective-permute-done.4
  34.7 3.5 %collective-permute-start.6 = (f32[384,256]{1,0:T(8,128)}, f32[384,256]{1,0:T(8,128)S(1)}, u32[]{:S(2)}, u32[]{:S(2)}) collective-permute-start(f32[384,256]{1,0:T(8,128)} %get-tuple-element.59.refs_0_), channel_id=1, source_target_pairs={{1,0},{2,1},{3,2},{0,3},{5,4},{6,5},{7,6},{4,7},{9,8},{10,9},{11,1... | collective-permute-start | bytes 1179656 | tf_op jit(solution)/shard_map/ppermute | solution.py:397
  38.3 1.4 collective-permute-start.7
  39.6 12.1 %shard_map.39 = (f32[256,256]{1,0:T(8,128)S(1)}, f32[256,256]{1,0:T(8,128)S(1)}, f32[256,256]{1,0:T(8,128)S(1)}) custom-call(f32[512,256]{1,0:T(8,128)S(1)} %get-tuple-element.56.mine, f32[512,256]{1,0:T(8,128)} %collective-permute-done.3.other), custom_call_target="tpu_custom_call" | custom-call | flops 16000000000 | bytes 1000000 | tf_op jit(solution)/shard_map/pallas_call | solution.py:470
  51.8 1.9 %shard_map.40 = (f32[256,256]{1,0:T(8,128)S(1)}, f32[1536,256]{1,0:T(8,128)S(1)}) custom-call(s32[768]{0:T(1024)S(1)} %get-tuple-element.98.idx_ref, f32[384,256]{1,0:T(8,128)} %get-tuple-element.59.refs_0_, f32[384,256]{1,0:T(8,128)S(1)} %collective-permute-done.6.refs_1_, f32[384,256]{1,0:T(8,128)S(1)} %collective-permute-done.7.refs_2_, ...), custom_call_target="tpu_custom_call" | custom-call | flops 3000000000 | bytes 3145728 | tf_op jit(solution)/shard_map/pallas_call | solution.py:425
  53.7 1.3 collective-permute-start.8
  55.0 1.6 collective-permute-start.22
  56.6 2.2 %collective-permute-start.10 = (f32[384,256]{1,0:T(8,128)S(1)}, f32[384,256]{1,0:T(8,128)S(1)}, u32[]{:S(2)}, u32[]{:S(2)}) collective-permute-start(f32[384,256]{1,0:T(8,128)S(1)} %copy-done.5), channel_id=1, source_target_pairs={{2,0},{3,1},{0,2},{1,3},{6,4},{7,5},{4,6},{5,7},{10,8},{11,9},{8,1... | collective-permute-start | bytes 1179656 | tf_op jit(solution)/shard_map/ppermute | solution.py:397
  58.9 12.6 %shard_map.41.inv = f32[512,512]{1,0:T(8,128)S(1)} custom-call(f32[256,256]{1,0:T(8,128)S(1)} %get-tuple-element.66.mine, f32[256,256]{1,0:T(8,128)S(1)} %collective-permute-done.8.other, f32[256,256]{1,0:T(8,128)S(1)} %get-tuple-element.58.inv, f32[256,256]{1,0:T(8,128)S(1)} %get-tuple-element.68.low, f32[256,256]{1,0:T(8,128)S(1)} %get-tuple-element.69.below), custom_call_target="tpu_custom_call" | custom-call | flops 16000000000 | bytes 1000000 | tf_op jit(solution)/shard_map/pallas_call | solution.py:478
  71.5 4.6 %collective-permute-done.10.refs_2_ = f32[384,256]{1,0:T(8,128)S(1)} collective-permute-done((f32[384,256]{1,0:T(8,128)S(1)}, f32[384,256]{1,0:T(8,128)S(1)}, u32[]{:S(2)}, u32[]{:S(2)}) %collective-permute-start.10) | collective-permute-done | bytes 393248 | tf_op jit(solution)/shard_map/ppermute | solution.py:397
  76.1 2.6 %shard_map.42 = (f32[768,256]{1,0:T(8,128)S(1)}, f32[1536,256]{1,0:T(8,128)S(1)}) custom-call(s32[768]{0:T(1024)S(1)} %get-tuple-element.98.idx_ref, f32[384,256]{1,0:T(8,128)S(1)} %copy-done.5, f32[384,256]{1,0:T(8,128)S(1)} %collective-permute-done.9.refs_1_, f32[384,256]{1,0:T(8,128)S(1)} %collective-permute-done.10.refs_2_, ...), custom_call_target="tpu_custom_call" | custom-call | flops 3000000000 | bytes 3145728 | tf_op jit(solution)/shard_map/pallas_call | solution.py:425
  78.8 1.8 %collective-permute-start.12 = (f32[768,256]{1,0:T(8,128)S(1)}, f32[768,256]{1,0:T(8,128)S(1)}, u32[]{:S(2)}, u32[]{:S(2)}) collective-permute-start(f32[768,256]{1,0:T(8,128)S(1)} %get-tuple-element.75.t_own), channel_id=1, source_target_pairs={{0,4},{4,0},{8,12},{12,8},{16,20},{20,16},{24,28},{28,24},{32,36},... | collective-permute-start | bytes 2359304 | tf_op jit(solution)/shard_map/ppermute | solution.py:393
  80.6 2.1 %collective-permute-done.22.refs_6_ = f32[384,768]{1,0:T(8,128)S(1)} collective-permute-done((f32[384,768]{1,0:T(8,128)S(1)}, f32[384,768]{1,0:T(8,128)S(1)}, u32[]{:S(2)}, u32[]{:S(2)}) %collective-permute-start.22) | collective-permute-done | bytes 1179680 | tf_op jit(solution)/shard_map/ppermute | solution.py:393
  82.8 0.8 collective-permute-start.27
  83.6 2.7 %collective-permute-start.23 = (f32[384,768]{1,0:T(8,128)S(1)}, f32[384,768]{1,0:T(8,128)S(1)}, u32[]{:S(2)}, u32[]{:S(2)}) collective-permute-start(f32[384,768]{1,0:T(8,128)S(1)} %collective-permute-done.22.refs_6_), channel_id=1, source_target_pairs={{1,0},{2,1},{3,2},{0,3},{5,4},{6,5},{7,6},{4,7},{9,8},{10,9},{11,1... | collective-permute-start | bytes 3538952 | tf_op jit(solution)/shard_map/ppermute | solution.py:397
  86.2 4.8 %shard_map.43 = (f32[512,512]{1,0:T(8,128)S(1)}, f32[256,512]{1,0:T(8,128)S(1)}, f32[256,256]{1,0:T(8,128)S(1)}, f32[128,256]{1,0:T(8,128)S(1)}) custom-call(s32[3]{0:T(128)S(1)} %pad_add_fusion.1.where, f32[512,512]{1,0:T(8,128)S(1)} %shard_map.41.inv, f32[768,256]{1,0:T(8,128)S(1)} %get-tuple-element.75.t_own, f32[768,256]{1,0:T(8,128)S(1)} %collective-permute-done.12.t_sib), custom_call_target="tpu_custom_call" | custom-call | flops 5000000000 | bytes 4194304 | tf_op jit(solution)/shard_map/pallas_call | solution.py:485
  91.0 1.5 collective-permute-start.13
  92.6 5.8 %collective-permute-done.13 = f32[256,256]{1,0:T(8,128)S(1)} collective-permute-done((f32[256,256]{1,0:T(8,128)S(1)}, f32[256,256]{1,0:T(8,128)S(1)}, u32[]{:S(2)}, u32[]{:S(2)}) %collective-permute-start.13) | collective-permute-done | bytes 262176 | tf_op jit(solution)/shard_map/ppermute | solution.py:393
  98.4 1.5 collective-permute-start.14
  99.9 2.7 %shard_map.44 = (f32[384,512]{1,0:T(8,128)S(1)}, f32[384,512]{1,0:T(8,128)S(1)}) custom-call(s32[3]{0:T(128)S(1)} %pad_add_fusion.1.where, f32[512,512]{1,0:T(8,128)S(1)} %shard_map.41.inv, f32[512,512]{1,0:T(8,128)S(1)} %get-tuple-element.79.m.m_ref, f32[384,768]{1,0:T(8,128)S(1)} %get-tuple-element.80.whole), custom_call_target="tpu_custom_call" | custom-call | flops 3000000000 | bytes 4194304 | tf_op jit(solution)/shard_map/pallas_call | solution.py:496
  102.6 2.2 %collective-permute-start.16 = (f32[256,256]{1,0:T(8,128)S(1)}, f32[256,256]{1,0:T(8,128)S(1)}, u32[]{:S(2)}, u32[]{:S(2)}) collective-permute-start(f32[256,256]{1,0:T(8,128)S(1)} %add.39.mine), channel_id=1, source_target_pairs={{0,4},{4,0},{8,12},{12,8},{16,20},{20,16},{24,28},{28,24},{32,36},... | collective-permute-start | bytes 786440 | tf_op jit(solution)/shard_map/ppermute | solution.py:393
  105.0 7.3 %collective-permute-done.24.refs_10_ = f32[384,768]{1,0:T(8,128)S(1)} collective-permute-done((f32[384,768]{1,0:T(8,128)S(1)}, f32[384,768]{1,0:T(8,128)S(1)}, u32[]{:S(2)}, u32[]{:S(2)}) %collective-permute-start.24) | collective-permute-done | bytes 1179680 | tf_op jit(solution)/shard_map/ppermute | solution.py:397
  112.3 0.9 collective-permute-start.20
  113.2 0.1 collective-permute-start.21
  113.4 2.7 %collective-permute-start.25 = (f32[192,768]{1,0:T(8,128)S(1)}, f32[192,768]{1,0:T(8,128)S(1)}, u32[]{:S(2)}, u32[]{:S(2)}) collective-permute-start(f32[192,768]{1,0:T(8,128)S(1)} %slice.8), channel_id=1, source_target_pairs={{1,0},{2,1},{3,2},{0,3},{5,4},{6,5},{7,6},{4,7},{9,8},{10,9},{11,1... | collective-permute-start | bytes 1769480 | tf_op jit(solution)/shard_map/ppermute | solution.py:397
  116.1 1.5 collective-permute-start.17
  117.7 11.6 %shard_map.45 = (f32[256,256]{1,0:T(8,128)S(1)}, f32[256,256]{1,0:T(8,128)S(1)}, f32[256,256]{1,0:T(8,128)S(1)}) custom-call(s32[3]{0:T(128)S(1)} %pad_add_fusion.1.where, f32[256,256]{1,0:T(8,128)S(1)} %add.39.mine, f32[256,256]{1,0:T(8,128)S(1)} %collective-permute-done.16.other), custom_call_target="tpu_custom_call" | custom-call | flops 16000000000 | bytes 1000000 | tf_op jit(solution)/shard_map/pallas_call | solution.py:505
  129.3 0.7 collective-permute-start.31
  130.0 0.1 collective-permute-start.28
  130.1 1.8 %collective-permute-done.26.refs_9_ = f32[192,768]{1,0:T(8,128)S(1)} collective-permute-done((f32[192,768]{1,0:T(8,128)S(1)}, f32[192,768]{1,0:T(8,128)S(1)}, u32[]{:S(2)}, u32[]{:S(2)}) %collective-permute-start.26) | collective-permute-done | bytes 589856 | tf_op jit(solution)/shard_map/ppermute | solution.py:397
  131.9 1.2 collective-permute-start.29
  133.2 0.4 collective-permute-start.18
  133.6 13.2 %shard_map.46.inv = f32[512,512]{1,0:T(8,128)S(1)} custom-call(s32[3]{0:T(128)S(1)} %pad_add_fusion.1.where, f32[128,256]{1,0:T(8,128)S(1)} %add.38.mine, f32[128,256]{1,0:T(8,128)S(1)} %collective-permute-done.15.other, f32[256,256]{1,0:T(8,128)S(1)} %get-tuple-element.83.inv, f32[256,256]{1,0:T(8,128)S(1)} %get-tuple-element.84.low, ...), custom_call_target="tpu_custom_call" | custom-call | flops 16000000000 | bytes 1000000 | tf_op jit(solution)/shard_map/pallas_call | solution.py:506
  146.9 0.9 copy-done.14
  147.8 0.4 copy-done.15
  148.2 24.5 %last.1 = f32[6144,384]{1,0:T(8,128)} custom-call(s32[3]{0:T(128)S(1)} %pad_add_fusion.1.where, f32[512,512]{1,0:T(8,128)S(1)} %shard_map.46.inv, f32[512,512]{1,0:T(8,128)} %copy-done.6, f32[256,512]{1,0:T(8,128)S(1)} %collective-permute-done.17.mz, f32[256,512]{1,0:T(8,128)S(1)} %collective-permute-done.18.mz_sib, f32[384,512]{1,0:T(8,128)S(1)} %get-tuple-element.81.gt, ...), custom_call_target="tpu_custom_call" | custom-call | flops 10000000000 | bytes 30000000 | tf_op jit(solution)/shard_map/last/pallas_call | solution.py:515
  (74 shorter events, 0.9 us)
Async XLA Ops:
  1.5 1.7 copy-start
  6.8 23.7 %copy-start.4 = (f32[384,256]{1,0:T(8,128)}, f32[384,256]{1,0:T(8,128)S(1)}, u32[]{:S(2)}) copy-start(f32[384,256]{1,0:T(8,128)S(1)} %get-tuple-element.71.refs_0_) | copy-start | bytes 1179652
  6.8 11.3 %collective-permute-start = (f32[384,256]{1,0:T(8,128)S(1)}, f32[384,256]{1,0:T(8,128)S(1)}, u32[]{:S(2)}, u32[]{:S(2)}) collective-permute-start(f32[384,256]{1,0:T(8,128)S(1)} %get-tuple-element.51.refs_0_), channel_id=1, source_target_pairs={{1,0},{2,1},{3,2},{0,3},{5,4},{6,5},{7,6},{4,7},{9,8},{10,9},{11,1... | collective-permute-start | bytes 1179656 | tf_op jit(solution)/shard_map/ppermute | solution.py:397
  10.4 11.8 %collective-permute-start.2 = (f32[384,256]{1,0:T(8,128)S(1)}, f32[384,256]{1,0:T(8,128)S(1)}, u32[]{:S(2)}, u32[]{:S(2)}) collective-permute-start(f32[384,256]{1,0:T(8,128)S(1)} %get-tuple-element.51.refs_0_), channel_id=1, source_target_pairs={{3,0},{0,1},{1,2},{2,3},{7,4},{4,5},{5,6},{6,7},{11,8},{8,9},{9,10... | collective-permute-start | bytes 1179656 | tf_op jit(solution)/shard_map/ppermute | solution.py:397
  18.2 10.3 %collective-permute-start.1 = (f32[384,256]{1,0:T(8,128)S(1)}, f32[384,256]{1,0:T(8,128)S(1)}, u32[]{:S(2)}, u32[]{:S(2)}) collective-permute-start(f32[384,256]{1,0:T(8,128)S(1)} %collective-permute-done.refs_1_), channel_id=1, source_target_pairs={{1,0},{2,1},{3,2},{0,3},{5,4},{6,5},{7,6},{4,7},{9,8},{10,9},{11,1... | collective-permute-start | bytes 1179656 | tf_op jit(solution)/shard_map/ppermute | solution.py:397
  22.1 16.1 %collective-permute-start.5 = (f32[384,256]{1,0:T(8,128)}, f32[384,256]{1,0:T(8,128)}, u32[]{:S(2)}, u32[]{:S(2)}) collective-permute-start(f32[384,256]{1,0:T(8,128)} %get-tuple-element.59.refs_0_), channel_id=1, source_target_pairs={{3,0},{0,1},{1,2},{2,3},{7,4},{4,5},{5,6},{6,7},{11,8},{8,9},{9,10... | collective-permute-start | bytes 1179656 | tf_op jit(solution)/shard_map/ppermute | solution.py:397
  30.5 50.0 %copy-start.1 = (f32[1536,256]{1,0:T(8,128)}, f32[1536,256]{1,0:T(8,128)S(1)}, u32[]{:S(2)}) copy-start(f32[1536,256]{1,0:T(8,128)S(1)} %get-tuple-element.91.refs_0_) | copy-start | bytes 4718596
  30.5 9.1 %collective-permute-start.3 = (f32[512,256]{1,0:T(8,128)S(1)}, f32[512,256]{1,0:T(8,128)}, u32[]{:S(2)}, u32[]{:S(2)}) collective-permute-start(f32[512,256]{1,0:T(8,128)S(1)} %get-tuple-element.56.mine), channel_id=1, source_target_pairs={{0,4},{4,0},{8,12},{12,8},{16,20},{20,16},{24,28},{28,24},{32,36},... | collective-permute-start | bytes 1572872 | tf_op jit(solution)/shard_map/ppermute | solution.py:393
  33.0 1.7 collective-permute-start.4
  34.7 17.1 %collective-permute-start.6 = (f32[384,256]{1,0:T(8,128)}, f32[384,256]{1,0:T(8,128)S(1)}, u32[]{:S(2)}, u32[]{:S(2)}) collective-permute-start(f32[384,256]{1,0:T(8,128)} %get-tuple-element.59.refs_0_), channel_id=1, source_target_pairs={{1,0},{2,1},{3,2},{0,3},{5,4},{6,5},{7,6},{4,7},{9,8},{10,9},{11,1... | collective-permute-start | bytes 1179656 | tf_op jit(solution)/shard_map/ppermute | solution.py:397
  38.2 20.7 %collective-permute-start.9 = (f32[384,256]{1,0:T(8,128)}, f32[384,256]{1,0:T(8,128)S(1)}, u32[]{:S(2)}, u32[]{:S(2)}) collective-permute-start(f32[384,256]{1,0:T(8,128)} %copy-done.4), channel_id=1, source_target_pairs={{1,0},{2,1},{3,2},{0,3},{5,4},{6,5},{7,6},{4,7},{9,8},{10,9},{11,1... | collective-permute-start | bytes 1179656 | tf_op jit(solution)/shard_map/ppermute | solution.py:397
  38.3 13.5 %collective-permute-start.7 = (f32[384,256]{1,0:T(8,128)}, f32[384,256]{1,0:T(8,128)S(1)}, u32[]{:S(2)}, u32[]{:S(2)}) collective-permute-start(f32[384,256]{1,0:T(8,128)} %collective-permute-done.5.refs_3_), channel_id=1, source_target_pairs={{3,0},{0,1},{1,2},{2,3},{7,4},{4,5},{5,6},{6,7},{11,8},{8,9},{9,10... | collective-permute-start | bytes 1179656 | tf_op jit(solution)/shard_map/ppermute | solution.py:397
  51.7 4.9 %copy-start.5 = (f32[384,256]{1,0:T(8,128)S(1)}, f32[384,256]{1,0:T(8,128)}, u32[]{:S(2)}) copy-start(f32[384,256]{1,0:T(8,128)} %copy-done.4) | copy-start | bytes 1179652
  53.7 58.6 %copy-start.2 = (f32[1536,256]{1,0:T(8,128)}, f32[1536,256]{1,0:T(8,128)S(1)}, u32[]{:S(2)}) copy-start(f32[1536,256]{1,0:T(8,128)S(1)} %get-tuple-element.92.refs_1_) | copy-start | bytes 4718596
  53.7 5.2 %collective-permute-start.8 = (f32[256,256]{1,0:T(8,128)S(1)}, f32[256,256]{1,0:T(8,128)S(1)}, u32[]{:S(2)}, u32[]{:S(2)}) collective-permute-start(f32[256,256]{1,0:T(8,128)S(1)} %get-tuple-element.66.mine), channel_id=1, source_target_pairs={{0,4},{4,0},{8,12},{12,8},{16,20},{20,16},{24,28},{28,24},{32,36},... | collective-permute-start | bytes 786440 | tf_op jit(solution)/shard_map/ppermute | solution.py:393
  55.0 27.8 %collective-permute-start.22 = (f32[384,768]{1,0:T(8,128)S(1)}, f32[384,768]{1,0:T(8,128)S(1)}, u32[]{:S(2)}, u32[]{:S(2)}) collective-permute-start(f32[384,768]{1,0:T(8,128)S(1)} %get-tuple-element.80.whole), channel_id=1, source_target_pairs={{0,8},{4,12},{8,0},{12,4},{16,24},{20,28},{24,16},{28,20},{32,40},... | collective-permute-start | bytes 3538952 | tf_op jit(solution)/shard_map/ppermute | solution.py:393
  56.6 14.9 %collective-permute-start.11 = (f32[384,256]{1,0:T(8,128)S(1)}, f32[384,256]{1,0:T(8,128)S(1)}, u32[]{:S(2)}, u32[]{:S(2)}) collective-permute-start(f32[384,256]{1,0:T(8,128)S(1)} %copy-done.5), channel_id=1, source_target_pairs={{3,0},{0,1},{1,2},{2,3},{7,4},{4,5},{5,6},{6,7},{11,8},{8,9},{9,10... | collective-permute-start | bytes 1179656 | tf_op jit(solution)/shard_map/ppermute | solution.py:397
  56.6 19.5 %collective-permute-start.10 = (f32[384,256]{1,0:T(8,128)S(1)}, f32[384,256]{1,0:T(8,128)S(1)}, u32[]{:S(2)}, u32[]{:S(2)}) collective-permute-start(f32[384,256]{1,0:T(8,128)S(1)} %copy-done.5), channel_id=1, source_target_pairs={{2,0},{3,1},{0,2},{1,3},{6,4},{7,5},{4,6},{5,7},{10,8},{11,9},{8,1... | collective-permute-start | bytes 1179656 | tf_op jit(solution)/shard_map/ppermute | solution.py:397
  78.8 34.4 %copy-start.3 = (f32[1536,256]{1,0:T(8,128)}, f32[1536,256]{1,0:T(8,128)S(1)}, u32[]{:S(2)}) copy-start(f32[1536,256]{1,0:T(8,128)S(1)} %get-tuple-element.93.refs_2_) | copy-start | bytes 4718596
  78.8 7.5 %collective-permute-start.12 = (f32[768,256]{1,0:T(8,128)S(1)}, f32[768,256]{1,0:T(8,128)S(1)}, u32[]{:S(2)}, u32[]{:S(2)}) collective-permute-start(f32[768,256]{1,0:T(8,128)S(1)} %get-tuple-element.75.t_own), channel_id=1, source_target_pairs={{0,4},{4,0},{8,12},{12,8},{16,20},{20,16},{24,28},{28,24},{32,36},... | collective-permute-start | bytes 2359304 | tf_op jit(solution)/shard_map/ppermute | solution.py:393
  80.5 32.9 %collective-permute-start.19 = (f32[1536,256]{1,0:T(8,128)S(1)}, f32[1536,256]{1,0:T(8,128)S(1)}, u32[]{:S(2)}, u32[]{:S(2)}) collective-permute-start(f32[1536,256]{1,0:T(8,128)S(1)} %get-tuple-element.91.refs_0_), channel_id=1, source_target_pairs={{0,4},{4,0},{8,12},{12,8},{16,20},{20,16},{24,28},{28,24},{32,36},... | collective-permute-start | bytes 4718600 | tf_op jit(solution)/shard_map/ppermute | solution.py:393
  82.8 8.2 %copy-start.12 = (f32[384,768]{1,0:T(8,128)}, f32[384,768]{1,0:T(8,128)S(1)}, u32[]{:S(2)}) copy-start(f32[384,768]{1,0:T(8,128)S(1)} %collective-permute-done.22.refs_6_) | copy-start | bytes 3538948
  82.8 22.1 %collective-permute-start.27 = (f32[384,768]{1,0:T(8,128)S(1)}, f32[384,768]{1,0:T(8,128)S(1)}, u32[]{:S(2)}, u32[]{:S(2)}) collective-permute-start(f32[384,768]{1,0:T(8,128)S(1)} %collective-permute-done.22.refs_6_), channel_id=1, source_target_pairs={{0,4},{4,0},{8,12},{12,8},{16,20},{20,16},{24,28},{28,24},{32,36},... | collective-permute-start | bytes 3538952 | tf_op jit(solution)/shard_map/ppermute | solution.py:393
  83.6 28.7 %collective-permute-start.24 = (f32[384,768]{1,0:T(8,128)S(1)}, f32[384,768]{1,0:T(8,128)S(1)}, u32[]{:S(2)}, u32[]{:S(2)}) collective-permute-start(f32[384,768]{1,0:T(8,128)S(1)} %collective-permute-done.22.refs_6_), channel_id=1, source_target_pairs={{3,0},{0,1},{1,2},{2,3},{7,4},{4,5},{5,6},{6,7},{11,8},{8,9},{9,10... | collective-permute-start | bytes 3538952 | tf_op jit(solution)/shard_map/ppermute | solution.py:397
  83.6 29.6 %collective-permute-start.23 = (f32[384,768]{1,0:T(8,128)S(1)}, f32[384,768]{1,0:T(8,128)S(1)}, u32[]{:S(2)}, u32[]{:S(2)}) collective-permute-start(f32[384,768]{1,0:T(8,128)S(1)} %collective-permute-done.22.refs_6_), channel_id=1, source_target_pairs={{1,0},{2,1},{3,2},{0,3},{5,4},{6,5},{7,6},{4,7},{9,8},{10,9},{11,1... | collective-permute-start | bytes 3538952 | tf_op jit(solution)/shard_map/ppermute | solution.py:397
  91.0 11.6 %copy-start.6 = (f32[512,512]{1,0:T(8,128)}, f32[512,512]{1,0:T(8,128)S(1)}, u32[]{:S(2)}) copy-start(f32[512,512]{1,0:T(8,128)S(1)} %get-tuple-element.79.m.m_ref) | copy-start | bytes 3145732
  91.0 7.4 %collective-permute-start.13 = (f32[256,256]{1,0:T(8,128)S(1)}, f32[256,256]{1,0:T(8,128)S(1)}, u32[]{:S(2)}, u32[]{:S(2)}) collective-permute-start(f32[256,256]{1,0:T(8,128)S(1)} %get-tuple-element.77), channel_id=1, source_target_pairs={{0,8},{4,12},{8,0},{12,4},{16,24},{20,28},{24,16},{28,20},{32,40},... | collective-permute-start | bytes 786440 | tf_op jit(solution)/shard_map/ppermute | solution.py:393
  98.4 4.2 %collective-permute-start.14 = (f32[128,256]{1,0:T(8,128)S(1)}, f32[128,256]{1,0:T(8,128)S(1)}, u32[]{:S(2)}, u32[]{:S(2)}) collective-permute-start(f32[128,256]{1,0:T(8,128)S(1)} %get-tuple-element.78), channel_id=1, source_target_pairs={{0,8},{4,12},{8,0},{12,4},{16,24},{20,28},{24,16},{28,20},{32,40},... | collective-permute-start | bytes 393224 | tf_op jit(solution)/shard_map/ppermute | solution.py:393
  102.6 13.5 %collective-permute-start.16 = (f32[256,256]{1,0:T(8,128)S(1)}, f32[256,256]{1,0:T(8,128)S(1)}, u32[]{:S(2)}, u32[]{:S(2)}) collective-permute-start(f32[256,256]{1,0:T(8,128)S(1)} %add.39.mine), channel_id=1, source_target_pairs={{0,4},{4,0},{8,12},{12,8},{16,20},{20,16},{24,28},{28,24},{32,36},... | collective-permute-start | bytes 786440 | tf_op jit(solution)/shard_map/ppermute | solution.py:393
  104.9 8.3 %copy-start.13 = (f32[384,768]{1,0:T(8,128)}, f32[384,768]{1,0:T(8,128)S(1)}, u32[]{:S(2)}) copy-start(f32[384,768]{1,0:T(8,128)S(1)} %collective-permute-done.27.refs_11_) | copy-start | bytes 3538948
  104.9 11.3 %collective-permute-start.15 = (f32[128,256]{1,0:T(8,128)S(1)}, f32[128,256]{1,0:T(8,128)S(1)}, u32[]{:S(2)}, u32[]{:S(2)}) collective-permute-start(f32[128,256]{1,0:T(8,128)S(1)} %add.38.mine), channel_id=1, source_target_pairs={{0,4},{4,0},{8,12},{12,8},{16,20},{20,16},{24,28},{28,24},{32,36},... | collective-permute-start | bytes 393224 | tf_op jit(solution)/shard_map/ppermute | solution.py:393
  112.3 17.0 %copy-start.7 = (f32[384,768]{1,0:T(8,128)}, f32[384,768]{1,0:T(8,128)S(1)}, u32[]{:S(2)}) copy-start(f32[384,768]{1,0:T(8,128)S(1)} %collective-permute-done.24.refs_10_) | copy-start | bytes 3538948
  112.3 17.0 %collective-permute-start.20 = (f32[1536,256]{1,0:T(8,128)S(1)}, f32[1536,256]{1,0:T(8,128)S(1)}, u32[]{:S(2)}, u32[]{:S(2)}) collective-permute-start(f32[1536,256]{1,0:T(8,128)S(1)} %get-tuple-element.92.refs_1_), channel_id=1, source_target_pairs={{0,4},{4,0},{8,12},{12,8},{16,20},{20,16},{24,28},{28,24},{32,36},... | collective-permute-start | bytes 4718600 | tf_op jit(solution)/shard_map/ppermute | solution.py:393
  113.2 16.8 %copy-start.8 = (f32[384,768]{1,0:T(8,128)}, f32[384,768]{1,0:T(8,128)S(1)}, u32[]{:S(2)}) copy-start(f32[384,768]{1,0:T(8,128)S(1)} %collective-permute-done.23.refs_7_) | copy-start | bytes 3538948
  113.2 19.9 %collective-permute-start.21 = (f32[1536,256]{1,0:T(8,128)S(1)}, f32[1536,256]{1,0:T(8,128)S(1)}, u32[]{:S(2)}, u32[]{:S(2)}) collective-permute-start(f32[1536,256]{1,0:T(8,128)S(1)} %get-tuple-element.93.refs_2_), channel_id=1, source_target_pairs={{0,4},{4,0},{8,12},{12,8},{16,20},{20,16},{24,28},{28,24},{32,36},... | collective-permute-start | bytes 4718600 | tf_op jit(solution)/shard_map/ppermute | solution.py:393
  113.4 2.7 %copy-start.9 = (f32[1536,256]{1,0:T(8,128)}, f32[1536,256]{1,0:T(8,128)S(1)}, u32[]{:S(2)}) copy-start(f32[1536,256]{1,0:T(8,128)S(1)} %collective-permute-done.19.refs_3_) | copy-start | bytes 4718596
  113.4 16.6 %collective-permute-start.25 = (f32[192,768]{1,0:T(8,128)S(1)}, f32[192,768]{1,0:T(8,128)S(1)}, u32[]{:S(2)}, u32[]{:S(2)}) collective-permute-start(f32[192,768]{1,0:T(8,128)S(1)} %slice.8), channel_id=1, source_target_pairs={{1,0},{2,1},{3,2},{0,3},{5,4},{6,5},{7,6},{4,7},{9,8},{10,9},{11,1... | collective-permute-start | bytes 1769480 | tf_op jit(solution)/shard_map/ppermute | solution.py:397
  116.1 15.8 %collective-permute-start.26 = (f32[192,768]{1,0:T(8,128)S(1)}, f32[192,768]{1,0:T(8,128)S(1)}, u32[]{:S(2)}, u32[]{:S(2)}) collective-permute-start(f32[192,768]{1,0:T(8,128)S(1)} %slice.9), channel_id=1, source_target_pairs={{3,0},{0,1},{1,2},{2,3},{7,4},{4,5},{5,6},{6,7},{11,8},{8,9},{9,10... | collective-permute-start | bytes 1769480 | tf_op jit(solution)/shard_map/ppermute | solution.py:397
  116.1 17.0 %collective-permute-start.17 = (f32[256,512]{1,0:T(8,128)S(1)}, f32[256,512]{1,0:T(8,128)S(1)}, u32[]{:S(2)}, u32[]{:S(2)}) collective-permute-start(f32[256,512]{1,0:T(8,128)S(1)} %get-tuple-element.87), channel_id=1, source_target_pairs={{0,8},{4,12},{8,0},{12,4},{16,24},{20,28},{24,16},{28,20},{32,40},... | collective-permute-start | bytes 1572872 | tf_op jit(solution)/shard_map/ppermute | solution.py:393
  129.3 17.5 %copy-start.10 = (f32[1536,256]{1,0:T(8,128)}, f32[1536,256]{1,0:T(8,128)S(1)}, u32[]{:S(2)}) copy-start(f32[1536,256]{1,0:T(8,128)S(1)} %collective-permute-done.20.refs_4_) | copy-start | bytes 4718596
  129.3 17.5 %collective-permute-start.31 = (f32[384,768]{1,0:T(8,128)S(1)}, f32[384,768]{1,0:T(8,128)S(1)}, u32[]{:S(2)}, u32[]{:S(2)}) collective-permute-start(f32[384,768]{1,0:T(8,128)S(1)} %collective-permute-done.24.refs_10_), channel_id=1, source_target_pairs={{0,4},{4,0},{8,12},{12,8},{16,20},{20,16},{24,28},{28,24},{32,36},... | collective-permute-start | bytes 3538952 | tf_op jit(solution)/shard_map/ppermute | solution.py:393
  130.0 16.9 %collective-permute-start.28 = (f32[384,768]{1,0:T(8,128)S(1)}, f32[384,768]{1,0:T(8,128)S(1)}, u32[]{:S(2)}, u32[]{:S(2)}) collective-permute-start(f32[384,768]{1,0:T(8,128)S(1)} %collective-permute-done.23.refs_7_), channel_id=1, source_target_pairs={{0,4},{4,0},{8,12},{12,8},{16,20},{20,16},{24,28},{28,24},{32,36},... | collective-permute-start | bytes 3538952 | tf_op jit(solution)/shard_map/ppermute | solution.py:393
  131.9 14.9 %collective-permute-start.29 = (f32[192,768]{1,0:T(8,128)S(1)}, f32[192,768]{1,0:T(8,128)S(1)}, u32[]{:S(2)}, u32[]{:S(2)}) collective-permute-start(f32[192,768]{1,0:T(8,128)S(1)} %collective-permute-done.25.refs_8_), channel_id=1, source_target_pairs={{0,4},{4,0},{8,12},{12,8},{16,20},{20,16},{24,28},{28,24},{32,36},... | collective-permute-start | bytes 1769480 | tf_op jit(solution)/shard_map/ppermute | solution.py:393
  133.1 13.7 %copy-start.11 = (f32[1536,256]{1,0:T(8,128)}, f32[1536,256]{1,0:T(8,128)S(1)}, u32[]{:S(2)}) copy-start(f32[1536,256]{1,0:T(8,128)S(1)} %collective-permute-done.21.refs_5_) | copy-start | bytes 4718596
  133.1 13.7 %collective-permute-start.30 = (f32[192,768]{1,0:T(8,128)S(1)}, f32[192,768]{1,0:T(8,128)S(1)}, u32[]{:S(2)}, u32[]{:S(2)}) collective-permute-start(f32[192,768]{1,0:T(8,128)S(1)} %collective-permute-done.26.refs_9_), channel_id=1, source_target_pairs={{0,4},{4,0},{8,12},{12,8},{16,20},{20,16},{24,28},{28,24},{32,36},... | collective-permute-start | bytes 1769480 | tf_op jit(solution)/shard_map/ppermute | solution.py:393
  133.2 13.7 %collective-permute-start.18 = (f32[256,512]{1,0:T(8,128)S(1)}, f32[256,512]{1,0:T(8,128)S(1)}, u32[]{:S(2)}, u32[]{:S(2)}) collective-permute-start(f32[256,512]{1,0:T(8,128)S(1)} %collective-permute-done.17.mz), channel_id=1, source_target_pairs={{0,4},{4,0},{8,12},{12,8},{16,20},{20,16},{24,28},{28,24},{32,36},... | collective-permute-start | bytes 1572872 | tf_op jit(solution)/shard_map/ppermute | solution.py:393
  146.8 1.0 copy-start.14
  146.8 1.4 copy-start.15

commit v2 on v1

--- a/solution.py
+++ b/solution.py
@@ -497,21 +497,25 @@
         side_kernel, (shape(w, IFACE),) * 2, 1, 3, 3 * 10**9, 2**22
     )(where, inv_one, m, whole)
     partz = farther_both(nearz, gt)
+    stack0, stack1, stack2, *near = after((stack0, stack1, stack2, *partz[:2], partz[4]), gt)
+    partz = near[0], near[1], partz[2], partz[3], near[2]
     ab = ab + after(ab_far, gt)
     ab_sib = swapped(ab, 1)
     d = after(d, ab_far)
     d = d + swapped(d, 2)
     d_sib = swapped(d, 1)
     half = call(half_two_kernel, (SQUARE,) * 3, 1, 2, HALF_COST, 10**6)(where, ab, ab_sib)
+    stacks = (stack0, stack1, stack2)
+    early = [swapped(v, 1) for v in (*stacks, partz[0], partz[1], partz[4])]
+    d_mine, d_other, early = after((d, d_sib, early))
     inv_two = call(
         whole_two_kernel, shape(IFACE, IFACE), 1, 5, HALF_COST, 10**6,
         [pltpu.VMEM((HALF, HALF), F32)],
-    )(where, d, d_sib, *half)
+    )(where, d_mine, d_other, *half)
 
     m_far = swapped(after(m_half, d), 2)
-    stacks = (stack0, stack1, stack2)
-    stacks_sib = [swapped(v, 1) for v in stacks]
-    partz_sib = [swapped(v, 1) for v in partz]
+    stacks_sib = early[:3]
+    partz_sib = early[3], early[4], swapped(partz[2], 1), swapped(partz[3], 1), early[5]
     out = pl.pallas_call(
         last_kernel,
         name="last",

time: 173 us -> 192 us (1.11)
  waiting for transfers between devices: 37.3 us -> 52.3 us
  starting transfers between devices: 38 us -> 41 us
    ppermute x13, waiting for transfers between devices: 27.9 us -> 37.3 us  [shifted(): lax.ppermute(shard, 'col', [((i + by) % COLS, i) for i in range(COLS)])]
    ppermute x19, waiting for transfers between devices: 9.42 us -> 15 us  [swapped(): return lax.ppermute(shard, 'box', [(i, i ^ apart) for i in range(n)])]
    ppermute x19, starting transfers between devices: 18.4 us -> 21.5 us  [swapped(): return lax.ppermute(shard, 'box', [(i, i ^ apart) for i in range(n)])]
  transfers between devices with their start and end apart: 32 -> 32, of which waited for: 8 -> 12; matrix products, arithmetic and copies ran while one was open for 0% -> 0% of each run, Pallas kernels for 37% -> 33%
where the time goes in v2:
time: 192 us; the launch traced here: 191 us
  Pallas kernels  91.6 us (48%)
  waiting for transfers between devices  52.3 us (27%)
  starting transfers between devices  41 us (21%)
  local copies, waits for them, and re-layouts  3.65 us (2%)
  other arithmetic  2.15 us (1%)
    ppermute x13, waiting for transfers between devices, shifted(): lax.ppermute(shard, 'col', [((i + by) % COLS, i) for i in range(COLS)])  37.3 us
    pallas_call x1, Pallas kernels, merged(): pl.pallas_call(last_kernel, name='last', out_shape=shape(COLS * boundary,...  24.5 us
    ppermute x19, starting transfers between devices, swapped(): return lax.ppermute(shard, 'box', [(i, i ^ apart) for i in range(n)])  21.5 us
    ppermute x13, starting transfers between devices, shifted(): lax.ppermute(shard, 'col', [((i + by) % COLS, i) for i in range(COLS)])  19.5 us
    ppermute x19, waiting for transfers between devices, swapped(): return lax.ppermute(shard, 'box', [(i, i ^ apart) for i in range(n)])  15 us
    pallas_call x1, Pallas kernels, merged(): call(whole_two_kernel, shape(IFACE, IFACE), 1, 5, HALF_COST, 10 ** 6, [pl...  13.2 us
    pallas_call x1, Pallas kernels, merged(): call(whole_one_kernel, shape(IFACE, IFACE), 0, 5, HALF_COST, 10 ** 6, [pl...  12.6 us
    pallas_call x1, Pallas kernels, merged(): call(half_one_kernel, (SQUARE,) * 3, 0, 2, HALF_COST, 10 ** 6)(t0, t0_sib)  12.1 us
  transfers between devices with their start and end apart: 32, of which 12 were waited for; matrix products, arithmetic and copies ran while one was open for 0% of the time, Pallas kernels for 33%

profile of v2, /device:TPU:1, one launch (start us, length us, event | category | flops | bytes accessed | tf_op | source)
XLA Modules:
  0.0 191.3 jit_solution(7160408062028040244)
XLA Ops:
  0.0 0.8 dynamic-slice_subtract_fusion
  0.8 0.7 pad_add_fusion
  1.5 1.7 copy-done
  3.2 3.7 %shard_map.37 = (f32[384,256]{1,0:T(8,128)S(1)}, f32[384,256]{1,0:T(8,128)}, f32[384,256]{1,0:T(8,128)S(1)}, f32[384,768]{1,0:T(8,128)S(1)}) custom-call(s32[768]{0:T(1024)S(1)} %get-tuple-element.125.idx_ref, f32[1536,384]{1,0:T(8,128)S(1)} %bitcast.8, s32[1,768]{1,0:T(1,128)S(1)} %broadcast_in_dim.11.list_ref), custom_call_target="tpu_custom_call" | custom-call | bytes 2359296 | tf_op jit(solution)/shard_map/pallas_call | solution.py:445
  6.8 0.7 copy-done.4
  7.6 3.6 %collective-permute-start = (f32[384,256]{1,0:T(8,128)S(1)}, f32[384,256]{1,0:T(8,128)S(1)}, u32[]{:S(2)}, u32[]{:S(2)}) collective-permute-start(f32[384,256]{1,0:T(8,128)S(1)} %get-tuple-element.65.refs_0_), channel_id=1, source_target_pairs={{1,0},{2,1},{3,2},{0,3},{5,4},{6,5},{7,6},{4,7},{9,8},{10,9},{11,1... | collective-permute-start | bytes 1179656 | tf_op jit(solution)/shard_map/ppermute | solution.py:397
  11.1 7.8 %collective-permute-done.refs_1_ = f32[384,256]{1,0:T(8,128)S(1)} collective-permute-done((f32[384,256]{1,0:T(8,128)S(1)}, f32[384,256]{1,0:T(8,128)S(1)}, u32[]{:S(2)}, u32[]{:S(2)}) %collective-permute-start) | collective-permute-done | bytes 393248 | tf_op jit(solution)/shard_map/ppermute | solution.py:397
  18.9 3.4 %collective-permute-start.1 = (f32[384,256]{1,0:T(8,128)S(1)}, f32[384,256]{1,0:T(8,128)S(1)}, u32[]{:S(2)}, u32[]{:S(2)}) collective-permute-start(f32[384,256]{1,0:T(8,128)S(1)} %collective-permute-done.refs_1_), channel_id=1, source_target_pairs={{1,0},{2,1},{3,2},{0,3},{5,4},{6,5},{7,6},{4,7},{9,8},{10,9},{11,1... | collective-permute-start | bytes 1179656 | tf_op jit(solution)/shard_map/ppermute | solution.py:397
  22.3 0.5 convert_reduce_fusion
  23.0 6.3 %collective-permute-done.1.refs_2_ = f32[384,256]{1,0:T(8,128)S(1)} collective-permute-done((f32[384,256]{1,0:T(8,128)S(1)}, f32[384,256]{1,0:T(8,128)S(1)}, u32[]{:S(2)}, u32[]{:S(2)}) %collective-permute-start.1) | collective-permute-done | bytes 393248 | tf_op jit(solution)/shard_map/ppermute | solution.py:397
  29.2 2.0 %shard_map.38 = (f32[512,256]{1,0:T(8,128)S(1)}, f32[1536,256]{1,0:T(8,128)S(1)}) custom-call(s32[768]{0:T(1024)S(1)} %get-tuple-element.126.idx_ref, f32[384,256]{1,0:T(8,128)S(1)} %get-tuple-element.65.refs_0_, f32[384,256]{1,0:T(8,128)S(1)} %collective-permute-done.refs_1_, f32[384,256]{1,0:T(8,128)S(1)} %collective-permute-done.1.refs_2_, ...), custom_call_target="tpu_custom_call" | custom-call | flops 3000000000 | bytes 3145728 | tf_op jit(solution)/shard_map/pallas_call | solution.py:425
  31.2 2.5 %collective-permute-start.3 = (f32[512,256]{1,0:T(8,128)S(1)}, f32[512,256]{1,0:T(8,128)}, u32[]{:S(2)}, u32[]{:S(2)}) collective-permute-start(f32[512,256]{1,0:T(8,128)S(1)} %get-tuple-element.70.mine), channel_id=1, source_target_pairs={{0,4},{4,0},{8,12},{12,8},{16,20},{20,16},{24,28},{28,24},{32,36},... | collective-permute-start | bytes 1572872 | tf_op jit(solution)/shard_map/ppermute | solution.py:393
  34.0 1.4 collective-permute-done.4
  35.4 3.5 %collective-permute-start.6 = (f32[384,256]{1,0:T(8,128)}, f32[384,256]{1,0:T(8,128)S(1)}, u32[]{:S(2)}, u32[]{:S(2)}) collective-permute-start(f32[384,256]{1,0:T(8,128)} %get-tuple-element.73.refs_0_), channel_id=1, source_target_pairs={{1,0},{2,1},{3,2},{0,3},{5,4},{6,5},{7,6},{4,7},{9,8},{10,9},{11,1... | collective-permute-start | bytes 1179656 | tf_op jit(solution)/shard_map/ppermute | solution.py:397
  39.0 1.4 collective-permute-start.7
  40.4 12.1 %shard_map.39 = (f32[256,256]{1,0:T(8,128)S(1)}, f32[256,256]{1,0:T(8,128)S(1)}, f32[256,256]{1,0:T(8,128)S(1)}) custom-call(f32[512,256]{1,0:T(8,128)S(1)} %get-tuple-element.70.mine, f32[512,256]{1,0:T(8,128)} %collective-permute-done.3.other), custom_call_target="tpu_custom_call" | custom-call | flops 16000000000 | bytes 1000000 | tf_op jit(solution)/shard_map/pallas_call | solution.py:470
  52.5 1.9 %shard_map.40 = (f32[256,256]{1,0:T(8,128)S(1)}, f32[1536,256]{1,0:T(8,128)S(1)}) custom-call(s32[768]{0:T(1024)S(1)} %get-tuple-element.126.idx_ref, f32[384,256]{1,0:T(8,128)} %get-tuple-element.73.refs_0_, f32[384,256]{1,0:T(8,128)S(1)} %collective-permute-done.6.refs_1_, f32[384,256]{1,0:T(8,128)S(1)} %collective-permute-done.7.refs_2_, ...), custom_call_target="tpu_custom_call" | custom-call | flops 3000000000 | bytes 3145728 | tf_op jit(solution)/shard_map/pallas_call | solution.py:425
  54.4 1.3 collective-permute-start.8
  55.7 1.6 collective-permute-start.16
  57.4 2.2 %collective-permute-start.10 = (f32[384,256]{1,0:T(8,128)S(1)}, f32[384,256]{1,0:T(8,128)S(1)}, u32[]{:S(2)}, u32[]{:S(2)}) collective-permute-start(f32[384,256]{1,0:T(8,128)S(1)} %copy-done.5), channel_id=1, source_target_pairs={{2,0},{3,1},{0,2},{1,3},{6,4},{7,5},{4,6},{5,7},{10,8},{11,9},{8,1... | collective-permute-start | bytes 1179656 | tf_op jit(solution)/shard_map/ppermute | solution.py:397
  59.6 12.6 %shard_map.41.inv = f32[512,512]{1,0:T(8,128)S(1)} custom-call(f32[256,256]{1,0:T(8,128)S(1)} %get-tuple-element.80.mine, f32[256,256]{1,0:T(8,128)S(1)} %collective-permute-done.8.other, f32[256,256]{1,0:T(8,128)S(1)} %get-tuple-element.72.inv, f32[256,256]{1,0:T(8,128)S(1)} %get-tuple-element.82.low, f32[256,256]{1,0:T(8,128)S(1)} %get-tuple-element.83.below), custom_call_target="tpu_custom_call" | custom-call | flops 16000000000 | bytes 1000000 | tf_op jit(solution)/shard_map/pallas_call | solution.py:478
  72.2 4.6 %collective-permute-done.10.refs_2_ = f32[384,256]{1,0:T(8,128)S(1)} collective-permute-done((f32[384,256]{1,0:T(8,128)S(1)}, f32[384,256]{1,0:T(8,128)S(1)}, u32[]{:S(2)}, u32[]{:S(2)}) %collective-permute-start.10) | collective-permute-done | bytes 393248 | tf_op jit(solution)/shard_map/ppermute | solution.py:397
  76.9 2.6 %shard_map.42 = (f32[768,256]{1,0:T(8,128)S(1)}, f32[1536,256]{1,0:T(8,128)S(1)}) custom-call(s32[768]{0:T(1024)S(1)} %get-tuple-element.126.idx_ref, f32[384,256]{1,0:T(8,128)S(1)} %copy-done.5, f32[384,256]{1,0:T(8,128)S(1)} %collective-permute-done.9.refs_1_, f32[384,256]{1,0:T(8,128)S(1)} %collective-permute-done.10.refs_2_, ...), custom_call_target="tpu_custom_call" | custom-call | flops 3000000000 | bytes 3145728 | tf_op jit(solution)/shard_map/pallas_call | solution.py:425
  79.5 1.8 collective-permute-start.12
  81.3 2.3 %collective-permute-done.16.refs_6_ = f32[384,768]{1,0:T(8,128)S(1)} collective-permute-done((f32[384,768]{1,0:T(8,128)S(1)}, f32[384,768]{1,0:T(8,128)S(1)}, u32[]{:S(2)}, u32[]{:S(2)}) %collective-permute-start.16) | collective-permute-done | bytes 1179680 | tf_op jit(solution)/shard_map/ppermute | solution.py:393
  83.5 2.7 %collective-permute-start.17 = (f32[384,768]{1,0:T(8,128)S(1)}, f32[384,768]{1,0:T(8,128)S(1)}, u32[]{:S(2)}, u32[]{:S(2)}) collective-permute-start(f32[384,768]{1,0:T(8,128)S(1)} %collective-permute-done.16.refs_6_), channel_id=1, source_target_pairs={{1,0},{2,1},{3,2},{0,3},{5,4},{6,5},{7,6},{4,7},{9,8},{10,9},{11,1... | collective-permute-start | bytes 3538952 | tf_op jit(solution)/shard_map/ppermute | solution.py:397
  86.2 4.8 %shard_map.43 = (f32[512,512]{1,0:T(8,128)S(1)}, f32[256,512]{1,0:T(8,128)S(1)}, f32[256,256]{1,0:T(8,128)S(1)}, f32[128,256]{1,0:T(8,128)S(1)}) custom-call(s32[3]{0:T(128)S(1)} %pad_add_fusion.1.where, f32[512,512]{1,0:T(8,128)S(1)} %shard_map.41.inv, f32[768,256]{1,0:T(8,128)S(1)} %get-tuple-element.89.t_own, f32[768,256]{1,0:T(8,128)S(1)} %collective-permute-done.12.t_sib), custom_call_target="tpu_custom_call" | custom-call | flops 5000000000 | bytes 4194304 | tf_op jit(solution)/shard_map/pallas_call | solution.py:485
  91.0 2.7 %shard_map.44 = (f32[384,512]{1,0:T(8,128)S(1)}, f32[384,512]{1,0:T(8,128)S(1)}) custom-call(s32[3]{0:T(128)S(1)} %pad_add_fusion.1.where, f32[512,512]{1,0:T(8,128)S(1)} %shard_map.41.inv, f32[512,512]{1,0:T(8,128)S(1)} %get-tuple-element.98.m.m_ref, f32[384,768]{1,0:T(8,128)S(1)} %get-tuple-element.96.whole), custom_call_target="tpu_custom_call" | custom-call | flops 3000000000 | bytes 4194304 | tf_op jit(solution)/shard_map/pallas_call | solution.py:496
  93.7 17.8 %collective-permute-done.18.refs_10_ = f32[384,768]{1,0:T(8,128)S(1)} collective-permute-done((f32[384,768]{1,0:T(8,128)S(1)}, f32[384,768]{1,0:T(8,128)S(1)}, u32[]{:S(2)}, u32[]{:S(2)}) %collective-permute-start.18) | collective-permute-done | bytes 1179680 | tf_op jit(solution)/shard_map/ppermute | solution.py:397
  111.5 1.7 collective-permute-start.22
  113.2 1.3 collective-permute-start.13
  114.6 2.7 %collective-permute-start.28 = (f32[192,768]{1,0:T(8,128)S(1)}, f32[192,768]{1,0:T(8,128)S(1)}, u32[]{:S(2)}, u32[]{:S(2)}) collective-permute-start(f32[192,768]{1,0:T(8,128)S(1)} %slice.8), channel_id=1, source_target_pairs={{1,0},{2,1},{3,2},{0,3},{5,4},{6,5},{7,6},{4,7},{9,8},{10,9},{11,1... | collective-permute-start | bytes 1769480 | tf_op jit(solution)/shard_map/ppermute | solution.py:397
  117.2 3.7 %collective-permute-done.13 = f32[256,256]{1,0:T(8,128)S(1)} collective-permute-done((f32[256,256]{1,0:T(8,128)S(1)}, f32[256,256]{1,0:T(8,128)S(1)}, u32[]{:S(2)}, u32[]{:S(2)}) %collective-permute-start.13) | collective-permute-done | bytes 262176 | tf_op jit(solution)/shard_map/ppermute | solution.py:393
  121.0 1.3 collective-permute-start.14
  122.3 2.8 %collective-permute-done.14 = f32[128,256]{1,0:T(8,128)S(1)} collective-permute-done((f32[128,256]{1,0:T(8,128)S(1)}, f32[128,256]{1,0:T(8,128)S(1)}, u32[]{:S(2)}, u32[]{:S(2)}) %collective-permute-start.14) | collective-permute-done | bytes 131104 | tf_op jit(solution)/shard_map/ppermute | solution.py:393
  125.1 1.4 collective-permute-start.26
  126.5 2.2 %collective-permute-start.25 = (f32[256,256]{1,0:T(8,128)S(1)}, f32[256,256]{1,0:T(8,128)S(1)}, u32[]{:S(2)}, u32[]{:S(2)}) collective-permute-start(f32[256,256]{1,0:T(8,128)S(1)} %add.39.mine), channel_id=1, source_target_pairs={{0,4},{4,0},{8,12},{12,8},{16,20},{20,16},{24,28},{28,24},{32,36},... | collective-permute-start | bytes 786440 | tf_op jit(solution)/shard_map/ppermute | solution.py:393
  128.7 1.2 collective-permute-done.25.other
  130.2 1.0 collective-permute-done.15.other
  131.9 0.8 collective-permute-done.29.refs_9_
  132.7 1.5 collective-permute-start.21
  134.2 2.7 %collective-permute-done.26.mz = f32[256,512]{1,0:T(8,128)S(1)} collective-permute-done((f32[256,512]{1,0:T(8,128)S(1)}, f32[256,512]{1,0:T(8,128)S(1)}, u32[]{:S(2)}, u32[]{:S(2)}) %collective-permute-start.26) | collective-permute-done | bytes 524320 | tf_op jit(solution)/shard_map/ppermute | solution.py:393
  136.9 2.7 %collective-permute-start.23 = (f32[384,768]{1,0:T(8,128)S(1)}, f32[384,768]{1,0:T(8,128)}, u32[]{:S(2)}, u32[]{:S(2)}) collective-permute-start(f32[384,768]{1,0:T(8,128)S(1)} %collective-permute-done.17.refs_7_), channel_id=1, source_target_pairs={{0,4},{4,0},{8,12},{12,8},{16,20},{20,16},{24,28},{28,24},{32,36},... | collective-permute-start | bytes 3538952 | tf_op jit(solution)/shard_map/ppermute | solution.py:393
  139.5 1.0 copy-done.13
  140.6 11.6 %shard_map.45 = (f32[256,256]{1,0:T(8,128)S(1)}, f32[256,256]{1,0:T(8,128)S(1)}, f32[256,256]{1,0:T(8,128)S(1)}) custom-call(s32[3]{0:T(128)S(1)} %pad_add_fusion.1.where, f32[256,256]{1,0:T(8,128)S(1)} %add.39.mine, f32[256,256]{1,0:T(8,128)S(1)} %collective-permute-done.25.other), custom_call_target="tpu_custom_call" | custom-call | flops 16000000000 | bytes 1000000 | tf_op jit(solution)/shard_map/pallas_call | solution.py:507
  152.2 0.6 collective-permute-start.30
  153.3 13.2 %shard_map.46.inv = f32[512,512]{1,0:T(8,128)S(1)} custom-call(s32[3]{0:T(128)S(1)} %pad_add_fusion.1.where, f32[128,256]{1,0:T(8,128)S(1)} %add.38.mine, f32[128,256]{1,0:T(8,128)S(1)} %collective-permute-done.15.other, f32[256,256]{1,0:T(8,128)S(1)} %get-tuple-element.109.inv, f32[256,256]{1,0:T(8,128)S(1)} %get-tuple-element.110.low, ...), custom_call_target="tpu_custom_call" | custom-call | flops 16000000000 | bytes 1000000 | tf_op jit(solution)/shard_map/pallas_call | solution.py:511
  166.5 24.5 %last.1 = f32[6144,384]{1,0:T(8,128)} custom-call(s32[3]{0:T(128)S(1)} %pad_add_fusion.1.where, f32[512,512]{1,0:T(8,128)S(1)} %shard_map.46.inv, f32[512,512]{1,0:T(8,128)} %copy-done.6, f32[256,512]{1,0:T(8,128)S(1)} %collective-permute-done.26.mz, f32[256,512]{1,0:T(8,128)S(1)} %collective-permute-done.27.mz_sib, f32[384,512]{1,0:T(8,128)S(1)} %get-tuple-element.99.gt, ...), custom_call_target="tpu_custom_call" | custom-call | flops 10000000000 | bytes 30000000 | tf_op jit(solution)/shard_map/last/pallas_call | solution.py:519
  (72 shorter events, 2.3 us)
Async XLA Ops:
  1.5 1.7 copy-start
  6.8 0.7 copy-start.4
  7.6 11.3 %collective-permute-start = (f32[384,256]{1,0:T(8,128)S(1)}, f32[384,256]{1,0:T(8,128)S(1)}, u32[]{:S(2)}, u32[]{:S(2)}) collective-permute-start(f32[384,256]{1,0:T(8,128)S(1)} %get-tuple-element.65.refs_0_), channel_id=1, source_target_pairs={{1,0},{2,1},{3,2},{0,3},{5,4},{6,5},{7,6},{4,7},{9,8},{10,9},{11,1... | collective-permute-start | bytes 1179656 | tf_op jit(solution)/shard_map/ppermute | solution.py:397
  11.1 11.8 %collective-permute-start.2 = (f32[384,256]{1,0:T(8,128)S(1)}, f32[384,256]{1,0:T(8,128)S(1)}, u32[]{:S(2)}, u32[]{:S(2)}) collective-permute-start(f32[384,256]{1,0:T(8,128)S(1)} %get-tuple-element.65.refs_0_), channel_id=1, source_target_pairs={{3,0},{0,1},{1,2},{2,3},{7,4},{4,5},{5,6},{6,7},{11,8},{8,9},{9,10... | collective-permute-start | bytes 1179656 | tf_op jit(solution)/shard_map/ppermute | solution.py:397
  18.9 10.3 %collective-permute-start.1 = (f32[384,256]{1,0:T(8,128)S(1)}, f32[384,256]{1,0:T(8,128)S(1)}, u32[]{:S(2)}, u32[]{:S(2)}) collective-permute-start(f32[384,256]{1,0:T(8,128)S(1)} %collective-permute-done.refs_1_), channel_id=1, source_target_pairs={{1,0},{2,1},{3,2},{0,3},{5,4},{6,5},{7,6},{4,7},{9,8},{10,9},{11,1... | collective-permute-start | bytes 1179656 | tf_op jit(solution)/shard_map/ppermute | solution.py:397
  22.8 16.1 %collective-permute-start.5 = (f32[384,256]{1,0:T(8,128)}, f32[384,256]{1,0:T(8,128)}, u32[]{:S(2)}, u32[]{:S(2)}) collective-permute-start(f32[384,256]{1,0:T(8,128)} %get-tuple-element.73.refs_0_), channel_id=1, source_target_pairs={{3,0},{0,1},{1,2},{2,3},{7,4},{4,5},{5,6},{6,7},{11,8},{8,9},{9,10... | collective-permute-start | bytes 1179656 | tf_op jit(solution)/shard_map/ppermute | solution.py:397
  31.2 100.0 %copy-start.1 = (f32[1536,256]{1,0:T(8,128)}, f32[1536,256]{1,0:T(8,128)S(1)}, u32[]{:S(2)}) copy-start(f32[1536,256]{1,0:T(8,128)S(1)} %get-tuple-element.100.refs_0_) | copy-start | bytes 4718596
  31.2 9.1 %collective-permute-start.3 = (f32[512,256]{1,0:T(8,128)S(1)}, f32[512,256]{1,0:T(8,128)}, u32[]{:S(2)}, u32[]{:S(2)}) collective-permute-start(f32[512,256]{1,0:T(8,128)S(1)} %get-tuple-element.70.mine), channel_id=1, source_target_pairs={{0,4},{4,0},{8,12},{12,8},{16,20},{20,16},{24,28},{28,24},{32,36},... | collective-permute-start | bytes 1572872 | tf_op jit(solution)/shard_map/ppermute | solution.py:393
  33.7 1.7 collective-permute-start.4
  35.4 17.1 %collective-permute-start.6 = (f32[384,256]{1,0:T(8,128)}, f32[384,256]{1,0:T(8,128)S(1)}, u32[]{:S(2)}, u32[]{:S(2)}) collective-permute-start(f32[384,256]{1,0:T(8,128)} %get-tuple-element.73.refs_0_), channel_id=1, source_target_pairs={{1,0},{2,1},{3,2},{0,3},{5,4},{6,5},{7,6},{4,7},{9,8},{10,9},{11,1... | collective-permute-start | bytes 1179656 | tf_op jit(solution)/shard_map/ppermute | solution.py:397
  38.9 20.7 %collective-permute-start.9 = (f32[384,256]{1,0:T(8,128)}, f32[384,256]{1,0:T(8,128)S(1)}, u32[]{:S(2)}, u32[]{:S(2)}) collective-permute-start(f32[384,256]{1,0:T(8,128)} %copy-done.4), channel_id=1, source_target_pairs={{1,0},{2,1},{3,2},{0,3},{5,4},{6,5},{7,6},{4,7},{9,8},{10,9},{11,1... | collective-permute-start | bytes 1179656 | tf_op jit(solution)/shard_map/ppermute | solution.py:397
  39.0 13.5 %collective-permute-start.7 = (f32[384,256]{1,0:T(8,128)}, f32[384,256]{1,0:T(8,128)S(1)}, u32[]{:S(2)}, u32[]{:S(2)}) collective-permute-start(f32[384,256]{1,0:T(8,128)} %collective-permute-done.5.refs_3_), channel_id=1, source_target_pairs={{3,0},{0,1},{1,2},{2,3},{7,4},{4,5},{5,6},{6,7},{11,8},{8,9},{9,10... | collective-permute-start | bytes 1179656 | tf_op jit(solution)/shard_map/ppermute | solution.py:397
  52.5 4.9 %copy-start.5 = (f32[384,256]{1,0:T(8,128)S(1)}, f32[384,256]{1,0:T(8,128)}, u32[]{:S(2)}) copy-start(f32[384,256]{1,0:T(8,128)} %copy-done.4) | copy-start | bytes 1179652
  54.4 77.2 %copy-start.2 = (f32[1536,256]{1,0:T(8,128)}, f32[1536,256]{1,0:T(8,128)S(1)}, u32[]{:S(2)}) copy-start(f32[1536,256]{1,0:T(8,128)S(1)} %get-tuple-element.101.refs_1_) | copy-start | bytes 4718596
  54.4 5.2 %collective-permute-start.8 = (f32[256,256]{1,0:T(8,128)S(1)}, f32[256,256]{1,0:T(8,128)S(1)}, u32[]{:S(2)}, u32[]{:S(2)}) collective-permute-start(f32[256,256]{1,0:T(8,128)S(1)} %get-tuple-element.80.mine), channel_id=1, source_target_pairs={{0,4},{4,0},{8,12},{12,8},{16,20},{20,16},{24,28},{28,24},{32,36},... | collective-permute-start | bytes 786440 | tf_op jit(solution)/shard_map/ppermute | solution.py:393
  55.7 27.8 %collective-permute-start.16 = (f32[384,768]{1,0:T(8,128)S(1)}, f32[384,768]{1,0:T(8,128)S(1)}, u32[]{:S(2)}, u32[]{:S(2)}) collective-permute-start(f32[384,768]{1,0:T(8,128)S(1)} %get-tuple-element.96.whole), channel_id=1, source_target_pairs={{0,8},{4,12},{8,0},{12,4},{16,24},{20,28},{24,16},{28,20},{32,40},... | collective-permute-start | bytes 3538952 | tf_op jit(solution)/shard_map/ppermute | solution.py:393
  57.4 14.9 %collective-permute-start.11 = (f32[384,256]{1,0:T(8,128)S(1)}, f32[384,256]{1,0:T(8,128)S(1)}, u32[]{:S(2)}, u32[]{:S(2)}) collective-permute-start(f32[384,256]{1,0:T(8,128)S(1)} %copy-done.5), channel_id=1, source_target_pairs={{3,0},{0,1},{1,2},{2,3},{7,4},{4,5},{5,6},{6,7},{11,8},{8,9},{9,10... | collective-permute-start | bytes 1179656 | tf_op jit(solution)/shard_map/ppermute | solution.py:397
  57.4 19.5 %collective-permute-start.10 = (f32[384,256]{1,0:T(8,128)S(1)}, f32[384,256]{1,0:T(8,128)S(1)}, u32[]{:S(2)}, u32[]{:S(2)}) collective-permute-start(f32[384,256]{1,0:T(8,128)S(1)} %copy-done.5), channel_id=1, source_target_pairs={{2,0},{3,1},{0,2},{1,3},{6,4},{7,5},{4,6},{5,7},{10,8},{11,9},{8,1... | collective-permute-start | bytes 1179656 | tf_op jit(solution)/shard_map/ppermute | solution.py:397
  79.5 53.2 %copy-start.3 = (f32[1536,256]{1,0:T(8,128)}, f32[1536,256]{1,0:T(8,128)S(1)}, u32[]{:S(2)}) copy-start(f32[1536,256]{1,0:T(8,128)S(1)} %get-tuple-element.102.refs_2_) | copy-start | bytes 4718596
  79.5 6.7 %collective-permute-start.12 = (f32[768,256]{1,0:T(8,128)S(1)}, f32[768,256]{1,0:T(8,128)S(1)}, u32[]{:S(2)}, u32[]{:S(2)}) collective-permute-start(f32[768,256]{1,0:T(8,128)S(1)} %get-tuple-element.89.t_own), channel_id=1, source_target_pairs={{0,4},{4,0},{8,12},{12,8},{16,20},{20,16},{24,28},{28,24},{32,36},... | collective-permute-start | bytes 2359304 | tf_op jit(solution)/shard_map/ppermute | solution.py:393
  83.5 28.0 %copy-start.12 = (f32[384,768]{1,0:T(8,128)}, f32[384,768]{1,0:T(8,128)S(1)}, u32[]{:S(2)}) copy-start(f32[384,768]{1,0:T(8,128)S(1)} %collective-permute-done.16.refs_6_) | copy-start | bytes 3538948
  83.5 28.0 %collective-permute-start.18 = (f32[384,768]{1,0:T(8,128)S(1)}, f32[384,768]{1,0:T(8,128)S(1)}, u32[]{:S(2)}, u32[]{:S(2)}) collective-permute-start(f32[384,768]{1,0:T(8,128)S(1)} %collective-permute-done.16.refs_6_), channel_id=1, source_target_pairs={{3,0},{0,1},{1,2},{2,3},{7,4},{4,5},{5,6},{6,7},{11,8},{8,9},{9,10... | collective-permute-start | bytes 3538952 | tf_op jit(solution)/shard_map/ppermute | solution.py:397
  83.5 28.0 %collective-permute-start.17 = (f32[384,768]{1,0:T(8,128)S(1)}, f32[384,768]{1,0:T(8,128)S(1)}, u32[]{:S(2)}, u32[]{:S(2)}) collective-permute-start(f32[384,768]{1,0:T(8,128)S(1)} %collective-permute-done.16.refs_6_), channel_id=1, source_target_pairs={{1,0},{2,1},{3,2},{0,3},{5,4},{6,5},{7,6},{4,7},{9,8},{10,9},{11,1... | collective-permute-start | bytes 3538952 | tf_op jit(solution)/shard_map/ppermute | solution.py:397
  91.0 2.7 %copy-start.6 = (f32[512,512]{1,0:T(8,128)}, f32[512,512]{1,0:T(8,128)S(1)}, u32[]{:S(2)}) copy-start(f32[512,512]{1,0:T(8,128)S(1)} %get-tuple-element.98.m.m_ref) | copy-start | bytes 3145732
  111.5 28.1 %copy-start.7 = (f32[384,768]{1,0:T(8,128)}, f32[384,768]{1,0:T(8,128)S(1)}, u32[]{:S(2)}) copy-start(f32[384,768]{1,0:T(8,128)S(1)} %collective-permute-done.18.refs_10_) | copy-start | bytes 3538948
  111.5 25.4 %copy-start.8 = (f32[384,768]{1,0:T(8,128)}, f32[384,768]{1,0:T(8,128)S(1)}, u32[]{:S(2)}) copy-start(f32[384,768]{1,0:T(8,128)S(1)} %collective-permute-done.17.refs_7_) | copy-start | bytes 3538948
  111.5 28.1 %collective-permute-start.22 = (f32[384,768]{1,0:T(8,128)S(1)}, f32[384,768]{1,0:T(8,128)S(1)}, u32[]{:S(2)}, u32[]{:S(2)}) collective-permute-start(f32[384,768]{1,0:T(8,128)S(1)} %collective-permute-done.16.refs_6_), channel_id=1, source_target_pairs={{0,4},{4,0},{8,12},{12,8},{16,20},{20,16},{24,28},{28,24},{32,36},... | collective-permute-start | bytes 3538952 | tf_op jit(solution)/shard_map/ppermute | solution.py:393
  113.2 7.8 %collective-permute-start.13 = (f32[256,256]{1,0:T(8,128)S(1)}, f32[256,256]{1,0:T(8,128)S(1)}, u32[]{:S(2)}, u32[]{:S(2)}) collective-permute-start(f32[256,256]{1,0:T(8,128)S(1)} %get-tuple-element.91), channel_id=1, source_target_pairs={{0,8},{4,12},{8,0},{12,4},{16,24},{20,28},{24,16},{28,20},{32,40},... | collective-permute-start | bytes 786440 | tf_op jit(solution)/shard_map/ppermute | solution.py:393
  114.6 17.0 %collective-permute-start.28 = (f32[192,768]{1,0:T(8,128)S(1)}, f32[192,768]{1,0:T(8,128)S(1)}, u32[]{:S(2)}, u32[]{:S(2)}) collective-permute-start(f32[192,768]{1,0:T(8,128)S(1)} %slice.8), channel_id=1, source_target_pairs={{1,0},{2,1},{3,2},{0,3},{5,4},{6,5},{7,6},{4,7},{9,8},{10,9},{11,1... | collective-permute-start | bytes 1769480 | tf_op jit(solution)/shard_map/ppermute | solution.py:397
  117.2 15.4 %collective-permute-start.29 = (f32[192,768]{1,0:T(8,128)S(1)}, f32[192,768]{1,0:T(8,128)S(1)}, u32[]{:S(2)}, u32[]{:S(2)}) collective-permute-start(f32[192,768]{1,0:T(8,128)S(1)} %slice.9), channel_id=1, source_target_pairs={{3,0},{0,1},{1,2},{2,3},{7,4},{4,5},{5,6},{6,7},{11,8},{8,9},{9,10... | collective-permute-start | bytes 1769480 | tf_op jit(solution)/shard_map/ppermute | solution.py:397
  121.0 4.1 %collective-permute-start.14 = (f32[128,256]{1,0:T(8,128)S(1)}, f32[128,256]{1,0:T(8,128)S(1)}, u32[]{:S(2)}, u32[]{:S(2)}) collective-permute-start(f32[128,256]{1,0:T(8,128)S(1)} %get-tuple-element.92), channel_id=1, source_target_pairs={{0,8},{4,12},{8,0},{12,4},{16,24},{20,28},{24,16},{28,20},{32,40},... | collective-permute-start | bytes 393224 | tf_op jit(solution)/shard_map/ppermute | solution.py:393
  125.1 11.8 %collective-permute-start.26 = (f32[256,512]{1,0:T(8,128)S(1)}, f32[256,512]{1,0:T(8,128)S(1)}, u32[]{:S(2)}, u32[]{:S(2)}) collective-permute-start(f32[256,512]{1,0:T(8,128)S(1)} %get-tuple-element.113), channel_id=1, source_target_pairs={{0,8},{4,12},{8,0},{12,4},{16,24},{20,28},{24,16},{28,20},{32,40},... | collective-permute-start | bytes 1572872 | tf_op jit(solution)/shard_map/ppermute | solution.py:393
  126.5 3.3 %collective-permute-start.25 = (f32[256,256]{1,0:T(8,128)S(1)}, f32[256,256]{1,0:T(8,128)S(1)}, u32[]{:S(2)}, u32[]{:S(2)}) collective-permute-start(f32[256,256]{1,0:T(8,128)S(1)} %add.39.mine), channel_id=1, source_target_pairs={{0,4},{4,0},{8,12},{12,8},{16,20},{20,16},{24,28},{28,24},{32,36},... | collective-permute-start | bytes 786440 | tf_op jit(solution)/shard_map/ppermute | solution.py:393
  129.9 1.4 collective-permute-start.15
  131.2 21.7 %collective-permute-start.19 = (f32[1536,256]{1,0:T(8,128)S(1)}, f32[1536,256]{1,0:T(8,128)S(1)}, u32[]{:S(2)}, u32[]{:S(2)}) collective-permute-start(f32[1536,256]{1,0:T(8,128)S(1)} %get-tuple-element.100.refs_0_), channel_id=1, source_target_pairs={{0,4},{4,0},{8,12},{12,8},{16,20},{20,16},{24,28},{28,24},{32,36},... | collective-permute-start | bytes 4718600 | tf_op jit(solution)/shard_map/ppermute | solution.py:393
  131.6 21.7 %collective-permute-start.20 = (f32[1536,256]{1,0:T(8,128)S(1)}, f32[1536,256]{1,0:T(8,128)S(1)}, u32[]{:S(2)}, u32[]{:S(2)}) collective-permute-start(f32[1536,256]{1,0:T(8,128)S(1)} %get-tuple-element.101.refs_1_), channel_id=1, source_target_pairs={{0,4},{4,0},{8,12},{12,8},{16,20},{20,16},{24,28},{28,24},{32,36},... | collective-permute-start | bytes 4718600 | tf_op jit(solution)/shard_map/ppermute | solution.py:393
  132.7 20.6 %collective-permute-start.21 = (f32[1536,256]{1,0:T(8,128)S(1)}, f32[1536,256]{1,0:T(8,128)S(1)}, u32[]{:S(2)}, u32[]{:S(2)}) collective-permute-start(f32[1536,256]{1,0:T(8,128)S(1)} %get-tuple-element.102.refs_2_), channel_id=1, source_target_pairs={{0,4},{4,0},{8,12},{12,8},{16,20},{20,16},{24,28},{28,24},{32,36},... | collective-permute-start | bytes 4718600 | tf_op jit(solution)/shard_map/ppermute | solution.py:393
  136.9 15.3 %collective-permute-start.23 = (f32[384,768]{1,0:T(8,128)S(1)}, f32[384,768]{1,0:T(8,128)}, u32[]{:S(2)}, u32[]{:S(2)}) collective-permute-start(f32[384,768]{1,0:T(8,128)S(1)} %collective-permute-done.17.refs_7_), channel_id=1, source_target_pairs={{0,4},{4,0},{8,12},{12,8},{16,20},{20,16},{24,28},{28,24},{32,36},... | collective-permute-start | bytes 3538952 | tf_op jit(solution)/shard_map/ppermute | solution.py:393
  139.5 1.0 copy-start.13
  140.6 12.2 %collective-permute-start.24 = (f32[384,768]{1,0:T(8,128)S(1)}, f32[384,768]{1,0:T(8,128)S(1)}, u32[]{:S(2)}, u32[]{:S(2)}) collective-permute-start(f32[384,768]{1,0:T(8,128)S(1)} %collective-permute-done.18.refs_10_), channel_id=1, source_target_pairs={{0,4},{4,0},{8,12},{12,8},{16,20},{20,16},{24,28},{28,24},{32,36},... | collective-permute-start | bytes 3538952 | tf_op jit(solution)/shard_map/ppermute | solution.py:393
  152.2 14.4 %collective-permute-start.30 = (f32[192,768]{1,0:T(8,128)S(1)}, f32[192,768]{1,0:T(8,128)S(1)}, u32[]{:S(2)}, u32[]{:S(2)}) collective-permute-start(f32[192,768]{1,0:T(8,128)S(1)} %collective-permute-done.28.refs_8_), channel_id=1, source_target_pairs={{0,4},{4,0},{8,12},{12,8},{16,20},{20,16},{24,28},{28,24},{32,36},... | collective-permute-start | bytes 1769480 | tf_op jit(solution)/shard_map/ppermute | solution.py:393
  152.8 13.7 %copy-start.14 = (f32[384,768]{1,0:T(8,128)}, f32[384,768]{1,0:T(8,128)S(1)}, u32[]{:S(2)}) copy-start(f32[384,768]{1,0:T(8,128)S(1)} %collective-permute-done.24.refs_15_) | copy-start | bytes 3538948
  152.8 13.8 %collective-permute-start.31 = (f32[192,768]{1,0:T(8,128)S(1)}, f32[192,768]{1,0:T(8,128)S(1)}, u32[]{:S(2)}, u32[]{:S(2)}) collective-permute-start(f32[192,768]{1,0:T(8,128)S(1)} %collective-permute-done.29.refs_9_), channel_id=1, source_target_pairs={{0,4},{4,0},{8,12},{12,8},{16,20},{20,16},{24,28},{28,24},{32,36},... | collective-permute-start | bytes 1769480 | tf_op jit(solution)/shard_map/ppermute | solution.py:393
  152.9 13.6 %copy-start.9 = (f32[1536,256]{1,0:T(8,128)}, f32[1536,256]{1,0:T(8,128)S(1)}, u32[]{:S(2)}) copy-start(f32[1536,256]{1,0:T(8,128)S(1)} %collective-permute-done.19.refs_3_) | copy-start | bytes 4718596
  152.9 13.7 %collective-permute-start.27 = (f32[256,512]{1,0:T(8,128)S(1)}, f32[256,512]{1,0:T(8,128)S(1)}, u32[]{:S(2)}, u32[]{:S(2)}) collective-permute-start(f32[256,512]{1,0:T(8,128)S(1)} %collective-permute-done.26.mz), channel_id=1, source_target_pairs={{0,4},{4,0},{8,12},{12,8},{16,20},{20,16},{24,28},{28,24},{32,36},... | collective-permute-start | bytes 1572872 | tf_op jit(solution)/shard_map/ppermute | solution.py:393
  153.3 13.2 %copy-start.10 = (f32[1536,256]{1,0:T(8,128)}, f32[1536,256]{1,0:T(8,128)S(1)}, u32[]{:S(2)}) copy-start(f32[1536,256]{1,0:T(8,128)S(1)} %collective-permute-done.20.refs_4_) | copy-start | bytes 4718596
  153.3 13.2 %copy-start.11 = (f32[1536,256]{1,0:T(8,128)}, f32[1536,256]{1,0:T(8,128)S(1)}, u32[]{:S(2)}) copy-start(f32[1536,256]{1,0:T(8,128)S(1)} %collective-permute-done.21.refs_5_) | copy-start | bytes 4718596
